TPU v7x, 512 devices: a whole 4x8x8 slice. The times are simulated.
512 devices in a mesh: dp: 32 (over x, y), fsdp: 16 (over z, core).
Axes of the slice: x: 4, y: 8, z: 8, core: 2. Of those that a mesh axis runs over, the one named last changes fastest.
Arguments:
- grad_partial: bfloat16 [32, 2, 1024, 8192], P('dp', None, 'fsdp'), may hold values from -0.25 to 0.25
- factors: float32 [32, 1024, 1024], P('dp', 'fsdp'), may hold values from -1 to 11, as said below
- bases: float32 [32, 1024, 1024], P('dp', 'fsdp'), may hold values from -1 to 2, as said below
- first_moment: float32 [32, 1024, 512], P('dp', 'fsdp'), may hold values from -0.3125 to 0.3125
- second_moment: float32 [32, 1024, 512], P('dp', 'fsdp'), may hold values from 0.003 to 0.03
Outputs:
- new_factors: float32 [32, 1024, 1024], P('dp', 'fsdp')
- new_bases: bfloat16 [32, 1024, 1024], P('dp', 'fsdp')
- new_first: float32 [32, 1024, 512], P('dp', 'fsdp')
- new_second: float32 [32, 1024, 512], P('dp', 'fsdp')
- direction: bfloat16 [32, 1024, 512], P('dp', 'fsdp')
Inputs may be any that keep to these rules, and one draw needn't show every extreme that they name: Each factors[t] is symmetric and positive definite. Each bases[t] is nonsingular.
All inputs are finite; a program needn't handle non-finite values.
Results may differ from a plain program's by a relative error of at most 0.024.
Values may be sent and summed in bfloat16 or wider, within the bound.
A program may use at most 64 MiB of HBM per device.

v0:
```python
import jax
import jax.numpy as jnp
from jax import lax
from jax.sharding import PartitionSpec as P


def swapped(block, axis, distance):
    count = lax.axis_size(axis)
    route = []
    for low in range(count):
        high = low | 1 << distance
        if high != low and high < count:
            route += [(low, high), (high, low)]
    return lax.ppermute(block, axis, route)


def ordered_halves(own_half, partner_half, side_bit):
    return jnp.where(
        side_bit == 0,
        jnp.concatenate([own_half, partner_half], axis=1),
        jnp.concatenate([partner_half, own_half], axis=1),
    )


def body(grad_partial, factors, bases, first_moment, second_moment):
    row_count = factors.shape[1]
    block_width = factors.shape[2]
    half_width = block_width // 2
    side_bit = lax.axis_index("dp") % 2
    row_start = lax.axis_index("fsdp") * row_count
    partial_rows = grad_partial[0]
    row_blocks = partial_rows.shape[0]
    column_blocks = partial_rows.shape[2] // block_width
    summand = partial_rows.reshape(row_blocks, row_count, column_blocks, 2, half_width).transpose(
        0, 2, 3, 1, 4
    )
    summand = summand.reshape(-1, half_width).astype(jnp.float32)
    grad_half = lax.psum_scatter(
        summand.astype(jnp.bfloat16), "dp", scatter_dimension=0, tiled=True
    )
    partner_half = swapped(grad_half, "dp", 0)
    own_rows = ordered_halves(grad_half, partner_half, side_bit)
    whole_block = lax.all_gather(own_rows, "fsdp", axis=0, tiled=True)

    def left_term():
        return lax.dot_general(
            own_rows, whole_block, (((1,), (1,)), ((), ())), preferred_element_type=jnp.float32
        )

    def right_term():
        column_rows = lax.dynamic_slice_in_dim(whole_block, row_start, row_count, 1)
        return lax.dot_general(
            column_rows, whole_block, (((0,), (0,)), ((), ())), preferred_element_type=jnp.float32
        )

    outer_term = lax.cond(side_bit == 0, left_term, right_term)
    new_factor = 0.95 * factors[0] + 0.05 * outer_term
    columns = new_factor
    power_rows = jnp.dot(
        columns,
        lax.all_gather(bases[0], "fsdp", axis=0, tiled=True),
        precision=lax.Precision.HIGHEST,
        preferred_element_type=jnp.float32,
    )
    gram_matrix = lax.psum(
        jnp.dot(
            power_rows.T,
            power_rows,
            precision=lax.Precision.HIGHEST,
            preferred_element_type=jnp.float32,
        ),
        "fsdp",
    )
    cholesky_factor = jnp.linalg.cholesky(gram_matrix)
    new_rows = lax.linalg.triangular_solve(
        cholesky_factor, power_rows, left_side=False, lower=True, transpose_a=True
    ).astype(jnp.bfloat16)
    partner_rows = swapped(new_rows, "dp", 0)
    left_rows = jnp.where(side_bit == 0, new_rows, partner_rows)
    right_rows = jnp.where(side_bit == 0, partner_rows, new_rows)
    left_full, right_full = (
        lax.all_gather(left_rows, "fsdp", axis=0, tiled=True),
        lax.all_gather(right_rows, "fsdp", axis=0, tiled=True),
    )
    left_columns = lax.dynamic_slice_in_dim(left_full, row_start, row_count, 1)
    mixed_rows = lax.dot_general(
        left_columns, whole_block, (((0,), (0,)), ((), ())), preferred_element_type=jnp.float32
    ).astype(jnp.bfloat16)
    right_half = lax.dynamic_slice_in_dim(right_full, side_bit * half_width, half_width, 1)
    rotated = jnp.dot(mixed_rows, right_half, preferred_element_type=jnp.float32)
    first_new = 0.95 * first_moment[0] + 0.05 * rotated
    second_new = 0.95 * second_moment[0] + 0.05 * rotated * rotated
    normalized = (first_new / (jnp.sqrt(second_new) + 1e-08)).astype(jnp.bfloat16)
    columns = left_rows
    weighted_half = jnp.dot(
        columns,
        lax.all_gather(normalized, "fsdp", axis=0, tiled=True),
        preferred_element_type=jnp.float32,
    ).astype(jnp.bfloat16)
    weighted_other = swapped(weighted_half, "dp", 0)
    weighted_rows = ordered_halves(weighted_half, weighted_other, side_bit)
    right_slice = lax.dynamic_slice_in_dim(right_full, side_bit * half_width, half_width, 0)
    combined = lax.dot_general(
        weighted_rows, right_slice, (((1,), (1,)), ((), ())), preferred_element_type=jnp.float32
    ).astype(jnp.bfloat16)
    return (new_factor[None], new_rows[None], first_new[None], second_new[None], combined[None])


def solution(mesh):
    return jax.shard_map(
        body,
        mesh=mesh,
        in_specs=(
            P("dp", None, "fsdp", None),
            P("dp", "fsdp", None),
            P("dp", "fsdp", None),
            P("dp", "fsdp", None),
            P("dp", "fsdp", None),
        ),
        out_specs=(
            P("dp", "fsdp", None),
            P("dp", "fsdp", None),
            P("dp", "fsdp", None),
            P("dp", "fsdp", None),
            P("dp", "fsdp", None),
        ),
        check_vma=False,
    )
```

profile of v0, /device:TPU:1, one launch (start us, length us, event | category | flops | bytes accessed | tf_op | source)
XLA Modules:
  0.0 966.1 jit_solution(8544133314279602019)
XLA Ops:
  7.2 3.3 reshape_squeeze.3
  10.5 2.5 copy.10
  13.1 224.5 %reduce-scatter.2.cloned.1.call-done = bf16[64,512]{1,0:T(8,128)(2,1)} async-done(((bf16[2048,512]{1,0:T(8,128)(2,1)}), bf16[64,512]{1,0:T(8,128)(2,1)}) %reduce-scatter.2.cloned.1.call-update) | async-done | bytes 65552 | tf_op jit(solution)/shard_map/reduce_scatter | solution.py:38
  237.6 2.0 collective-permute-start
  239.6 3.2 collective-permute-done
  242.8 1.6 maximum_select_fusion
  245.2 47.6 %all-gather.7.cloned.1.call-done = bf16[1024,1024]{1,0:T(8,128)(2,1)} async-done(((bf16[64,1024]{1,0:T(8,128)(2,1)}), bf16[1024,1024]{1,0:T(8,128)(2,1)}) %all-gather.7.cloned.1.call-update) | async-done | bytes 2097168 | tf_op jit(solution)/shard_map/all_gather | solution.py:43
  292.8 2.4 conditional.1
  292.8 2.4 fusion.93
  295.2 43.0 %all-gather.15.cloned.1.call-done = f32[1,1024,1024]{2,1,0:T(8,128)} async-done(((f32[1,64,1024]{2,1,0:T(8,128)}), f32[1,1024,1024]{2,1,0:T(8,128)}) %all-gather.15.cloned.1.call-update) | async-done | bytes 4194320 | tf_op jit(solution)/shard_map/all_gather | solution.py:61
  338.2 4.8 fusion.4
  343.0 5.1 fusion.94
  348.2 125.0 %all-reduce.3.cloned.1.call-done = f32[1024,1024]{0,1:T(8,128)} async-done(((f32[1024,1024]{0,1:T(8,128)}), f32[1024,1024]{0,1:T(8,128)}) %all-reduce.3.cloned.1.call-update) | async-done | bytes 4194320 | tf_op jit(solution)/shard_map/psum | solution.py:65
  473.2 5.6 copy.12
  478.8 4.4 fusion.3
  483.3 1.9 copy-done.1
  485.2 11.7 %cholesky.223 = f32[128,128]{1,0:T(8,128)S(1)} custom-call(f32[128,128]{1,0:T(8,128)S(1)} %cholesky.580), custom_call_target="Cholesky" | custom-call | tf_op jit(solution)/shard_map/jit(cholesky)/cholesky | solution.py:74
  497.0 2.5 cholesky.255
  499.5 9.8 %custom-call.62 = f32[1,128,128]{1,2,0:T(8,128)S(1)} custom-call(f32[1,128,128]{2,1,0:T(8,128)S(1)} %get-tuple-element.64), custom_call_target="InvertDiagBlocksLowerTriangular" | custom-call | tf_op jit(solution)/shard_map/jit(cholesky)/cholesky | solution.py:74
  509.3 2.4 constant_dynamic-update-slice_fusion.38
  511.7 1.5 convolution_subtract_fusion
  513.2 12.2 %cholesky.244 = f32[128,128]{1,0:T(8,128)S(1)} custom-call(f32[128,128]{1,0:T(8,128)S(1)} %cholesky.584), custom_call_target="Cholesky" | custom-call | tf_op jit(solution)/shard_map/jit(cholesky)/cholesky | solution.py:74
  526.1 9.8 %custom-call.63 = f32[1,128,128]{1,2,0:T(8,128)S(1)} custom-call(f32[1,128,128]{2,1,0:T(8,128)S(1)} %get-tuple-element.61), custom_call_target="InvertDiagBlocksLowerTriangular" | custom-call | tf_op jit(solution)/shard_map/jit(cholesky)/cholesky | solution.py:74
  537.1 2.1 convolution_subtract_fusion.1
  539.2 11.7 %cholesky.468 = f32[128,128]{1,0:T(8,128)S(1)} custom-call(f32[128,128]{1,0:T(8,128)S(1)} %cholesky.589), custom_call_target="Cholesky" | custom-call | tf_op jit(solution)/shard_map/jit(cholesky)/cholesky | solution.py:74
  552.2 9.8 %custom-call.64 = f32[1,128,128]{1,2,0:T(8,128)S(1)} custom-call(f32[1,128,128]{2,1,0:T(8,128)S(1)} %get-tuple-element.58), custom_call_target="InvertDiagBlocksLowerTriangular" | custom-call | tf_op jit(solution)/shard_map/jit(cholesky)/cholesky | solution.py:74
  563.2 2.3 convolution_subtract_fusion.2
  565.6 11.8 %cholesky.487 = f32[128,128]{1,0:T(8,128)S(1)} custom-call(f32[128,128]{1,0:T(8,128)S(1)} %cholesky.594), custom_call_target="Cholesky" | custom-call | tf_op jit(solution)/shard_map/jit(cholesky)/cholesky | solution.py:74
  578.7 9.8 %custom-call.65 = f32[1,128,128]{1,2,0:T(8,128)S(1)} custom-call(f32[1,128,128]{2,1,0:T(8,128)S(1)} %get-tuple-element.55), custom_call_target="InvertDiagBlocksLowerTriangular" | custom-call | tf_op jit(solution)/shard_map/jit(cholesky)/cholesky | solution.py:74
  589.7 2.3 convolution_subtract_fusion.3
  592.0 11.7 %cholesky.506 = f32[128,128]{1,0:T(8,128)S(1)} custom-call(f32[128,128]{1,0:T(8,128)S(1)} %cholesky.599), custom_call_target="Cholesky" | custom-call | tf_op jit(solution)/shard_map/jit(cholesky)/cholesky | solution.py:74
  605.1 10.0 %custom-call.66 = f32[1,128,128]{1,2,0:T(8,128)S(1)} custom-call(f32[1,128,128]{2,1,0:T(8,128)S(1)} %get-tuple-element.52), custom_call_target="InvertDiagBlocksLowerTriangular" | custom-call | tf_op jit(solution)/shard_map/jit(cholesky)/cholesky | solution.py:74
  616.1 2.3 convolution_subtract_fusion.4
  618.4 11.7 %cholesky.526 = f32[128,128]{1,0:T(8,128)S(1)} custom-call(f32[128,128]{1,0:T(8,128)S(1)} %cholesky.604), custom_call_target="Cholesky" | custom-call | tf_op jit(solution)/shard_map/jit(cholesky)/cholesky | solution.py:74
  631.4 9.8 %custom-call.67 = f32[1,128,128]{1,2,0:T(8,128)S(1)} custom-call(f32[1,128,128]{2,1,0:T(8,128)S(1)} %get-tuple-element.49), custom_call_target="InvertDiagBlocksLowerTriangular" | custom-call | tf_op jit(solution)/shard_map/jit(cholesky)/cholesky | solution.py:74
  642.1 2.0 convolution_subtract_fusion.5
  644.2 12.1 %cholesky.546 = f32[128,128]{1,0:T(8,128)S(1)} custom-call(f32[128,128]{1,0:T(8,128)S(1)} %cholesky.609), custom_call_target="Cholesky" | custom-call | tf_op jit(solution)/shard_map/jit(cholesky)/cholesky | solution.py:74
  657.6 9.8 %custom-call.68 = f32[1,128,128]{1,2,0:T(8,128)S(1)} custom-call(f32[1,128,128]{2,1,0:T(8,128)S(1)} %get-tuple-element.46), custom_call_target="InvertDiagBlocksLowerTriangular" | custom-call | tf_op jit(solution)/shard_map/jit(cholesky)/cholesky | solution.py:74
  668.2 1.9 convolution_subtract_fusion.6
  670.1 11.7 %cholesky.564 = f32[128,128]{1,0:T(8,128)S(1)} custom-call(f32[128,128]{1,0:T(8,128)S(1)} %convolution_subtract_fusion.6), custom_call_target="Cholesky" | custom-call | tf_op jit(solution)/shard_map/jit(cholesky)/cholesky | solution.py:74
  688.7 4.8 select_select_fusion
  693.5 28.1 %while.1 = (s32[]{:T(128)}, f32[1024,1024]{1,0:T(8,128)}, s32[8,2]{0,1:T(2,128)S(1)}, f32[8,128,128]{2,1,0:T(8,128)}, s32[]{:T(128)}) while((s32[]{:T(128)}, f32[1024,1024]{1,0:T(8,128)}, s32[8,2]{0,1:T(2,128)S(1)}, f32[8,128,128]{2,1,0:T(8,128)}, s32[]{:T(128)}) %tuple.69), condition=%wide.while_cond, body=%wide.while_body.sunk | while | flops 2 | bytes 132705 | solution.py:75
  694.1 3.0 bitcast_dynamic-update-slice_fusion.2
  697.7 2.9 bitcast_dynamic-update-slice_fusion.2
  701.2 2.9 bitcast_dynamic-update-slice_fusion.2
  704.7 2.9 bitcast_dynamic-update-slice_fusion.2
  708.2 2.9 bitcast_dynamic-update-slice_fusion.2
  711.7 2.9 bitcast_dynamic-update-slice_fusion.2
  715.2 2.9 bitcast_dynamic-update-slice_fusion.2
  718.8 2.9 bitcast_dynamic-update-slice_fusion.2
  721.6 79.6 %custom-call.69 = f32[8,128,128]{1,2,0:T(8,128)S(1)} custom-call(f32[8,128,128]{2,1,0:T(8,128)} %get-tuple-element.27), custom_call_target="InvertDiagBlocksLowerTriangular" | custom-call | tf_op jit(solution)/shard_map/triangular_solve | solution.py:75
  805.6 1.3 convolution_subtract_fusion.13
  807.3 1.5 convolution_subtract_fusion.12
  809.0 1.5 convolution_subtract_fusion.11
  810.7 1.7 convolution_subtract_fusion.7
  812.6 3.1 collective-permute-start.1
  815.7 2.6 collective-permute-done.1
  819.7 43.9 %all-gather.11.cloned.1.call-done = bf16[1024,1024]{1,0:T(8,128)(2,1)} async-done(((bf16[64,1024]{1,0:T(8,128)(2,1)}), bf16[1024,1024]{1,0:T(8,128)(2,1)}) %all-gather.11.cloned.1.call-update) | async-done | bytes 2097168 | tf_op jit(solution)/shard_map/all_gather | solution.py:83
  863.7 43.5 %all-gather.9.cloned.1.call-done = bf16[1024,1024]{1,0:T(8,128)(2,1)} async-done(((bf16[64,1024]{1,0:T(8,128)(2,1)}), bf16[1024,1024]{1,0:T(8,128)(2,1)}) %all-gather.9.cloned.1.call-update) | async-done | bytes 2097168 | tf_op jit(solution)/shard_map/all_gather | solution.py:82
  907.2 2.9 divide_convert_fusion
  910.1 40.1 %all-gather.13.cloned.1.call-done = bf16[1024,512]{1,0:T(8,128)(2,1)} async-done(((bf16[64,512]{1,0:T(8,128)(2,1)}), bf16[1024,512]{1,0:T(8,128)(2,1)}) %all-gather.13.cloned.1.call-update) | async-done | bytes 1048592 | tf_op jit(solution)/shard_map/all_gather | solution.py:97
  950.2 1.5 convolution_convert_fusion.2
  951.8 3.1 collective-permute-start.2
  956.8 2.3 fusion.7
  (101 shorter events, 29.7 us)
Async XLA Ops:
  7.2 230.4 %reduce-scatter.2.cloned.1.call-start = ((), (), s32[]{:S(2)}) async-start(), calls=%async_computation.1 | async-start | bytes 2162688 | tf_op jit(solution)/shard_map/reduce_scatter | solution.py:38
  13.0 325.2 %copy-start.3 = (f32[1,64,1024]{2,1,0:T(8,128)S(1)}, f32[1,64,1024]{2,1,0:T(8,128)}, u32[]{:S(2)}) copy-start(f32[1,64,1024]{2,1,0:T(8,128)} %param.8) | copy-start | bytes 786436
  13.1 279.8 %all-gather.7.cloned.1.call-start = ((), (), s32[]{:S(2)}) async-start(), calls=%async_computation.2 | async-start | bytes 2228224 | tf_op jit(solution)/shard_map/all_gather | solution.py:43
  237.6 5.2 collective-permute-start
  244.4 93.8 %all-gather.15.cloned.1.call-start = ((), (), s32[]{:S(2)}) async-start(), calls=%async_computation.7 | async-start | bytes 4456448 | tf_op jit(solution)/shard_map/all_gather | solution.py:61
  245.2 228.0 %all-reduce.3.cloned.1.call-start = ((), (), s32[]{:S(2)}) async-start(), calls=%async_computation.3 | async-start | bytes 8388608 | tf_op jit(solution)/shard_map/psum | solution.py:65
  348.1 515.5 %all-gather.11.cloned.1.call-start = ((), (), s32[]{:S(2)}) async-start(), calls=%async_computation.5 | async-start | bytes 2228224 | tf_op jit(solution)/shard_map/all_gather | solution.py:83
  483.3 1.9 copy-start.1
  693.5 213.7 %copy-start = (bf16[1024,1024]{1,0:T(8,128)(2,1)S(1)}, bf16[1024,1024]{1,0:T(8,128)(2,1)}, u32[]{:S(2)}) copy-start(bf16[1024,1024]{1,0:T(8,128)(2,1)} %all-gather.7.cloned.1.call-done) | copy-start | bytes 6291460
  693.5 213.7 %copy-start.4 = (f32[1,64,512]{2,1,0:T(8,128)S(1)}, f32[1,64,512]{2,1,0:T(8,128)}, u32[]{:S(2)}) copy-start(f32[1,64,512]{2,1,0:T(8,128)} %param.10) | copy-start | bytes 393220
  812.6 6.5 copy-start.5
  812.6 5.7 collective-permute-start.1
  819.1 131.2 %copy-start.2 = (bf16[64,1024]{1,0:T(8,128)(2,1)S(1)}, bf16[64,1024]{1,0:T(8,128)(2,1)}, u32[]{:S(2)}) copy-start(bf16[64,1024]{1,0:T(8,128)(2,1)} %get-tuple-element.41) | copy-start | bytes 393220
  819.1 88.1 %all-gather.9.cloned.1.call-start = ((), (), s32[]{:S(2)}) async-start(), calls=%async_computation.4 | async-start | bytes 2228224 | tf_op jit(solution)/shard_map/all_gather | solution.py:82
  819.7 130.6 %all-gather.13.cloned.1.call-start = ((), (), s32[]{:S(2)}) async-start(), calls=%async_computation.6 | async-start | bytes 1114112 | tf_op jit(solution)/shard_map/all_gather | solution.py:97
  951.8 5.0 collective-permute-start.2
Sparse Core Ops, SparseCore 0:
  13.2 224.3 reduce-scatter.1
  244.5 48.2 all-gather.6
  294.9 43.2 all-gather.14
  348.2 124.8 all-reduce.2
  819.2 44.4 all-gather.10
  866.2 40.9 all-gather.8
  910.2 39.9 all-gather.12
where the time goes:
time: 973 us; the launch traced here: 966 us
  waiting for transfers between devices  576 us (59%)
  other arithmetic  265 us (27%)
  matrix products  53.3 us (5%)
  local copies, waits for them, and re-layouts  44.1 us (5%)
  between operations  19.8 us (2%)
    reduce_scatter x1, waiting for transfers between devices, body(): lax.psum_scatter(summand.astype(jnp.bfloat16), 'dp', scatter_dimension=0,...  224 us
    another operation x30, other arithmetic, body(): cholesky_factor = jnp.linalg.cholesky(gram_matrix)  173 us
    psum x1, waiting for transfers between devices, body(): lax.psum(jnp.dot(power_rows.T, power_rows, precision=lax.Precision.HIGHES...  125 us
    another operation x3, other arithmetic, body(): lax.linalg.triangular_solve(cholesky_factor, power_rows, left_side=False,...  84.4 us
    all_gather x1, waiting for transfers between devices, body(): whole_block = lax.all_gather(own_rows, 'fsdp', axis=0, tiled=True)  47.6 us
    all_gather x1, waiting for transfers between devices, body(): lax.all_gather(right_rows, 'fsdp', axis=0, tiled=True)  43.9 us
    all_gather x1, waiting for transfers between devices, body(): lax.all_gather(left_rows, 'fsdp', axis=0, tiled=True)  43.5 us
    all_gather x1, waiting for transfers between devices, body(): lax.all_gather(bases[0], 'fsdp', axis=0, tiled=True)  43 us
  transfers between devices with their start and end apart: 10, of which 10 were waited for; matrix products, arithmetic and copies ran while one was open for 0% of the time, Pallas kernels for 0%

commit v1 on v0

v1 whole, which is shorter than its diff:
```python
import functools

import jax
import jax.numpy as jnp
from jax import lax
from jax.experimental import pallas as pl
from jax.experimental.pallas import tpu as pltpu
from jax.sharding import PartitionSpec as P

F32 = jnp.float32
BF16 = jnp.bfloat16
NN = (((1,), (0,)), ((), ()))
NT = (((1,), (1,)), ((), ()))
TN = (((0,), (0,)), ((), ()))
NX, NY, NZ = 4, 8, 8
ROWS = 64
BLOCK = 1024
HALF = 512
CHUNKS = 4
CROWS = ROWS // CHUNKS
PANEL = 128
VMEM_SPEC = pl.BlockSpec(memory_space=pltpu.VMEM)
VMEM_BYTES = 60 << 20


def place():
    dp = lax.axis_index("dp")
    fsdp = lax.axis_index("fsdp")
    return dp // NY, lax.rem(dp, NY), fsdp // 2, lax.rem(fsdp, 2)


def remote(src, dst, send, recv, dp, fsdp):
    return pltpu.make_async_remote_copy(
        src_ref=src,
        dst_ref=dst,
        send_sem=send,
        recv_sem=recv,
        device_id={"dp": dp, "fsdp": fsdp},
        device_id_type=pl.DeviceIdType.MESH,
    )


def meet(peers):
    barrier = pltpu.get_barrier_semaphore()
    for dp, fsdp in peers:
        pl.semaphore_signal(
            barrier,
            inc=1,
            device_id={"dp": dp, "fsdp": fsdp},
            device_id_type=pl.DeviceIdType.MESH,
        )
    pl.semaphore_wait(barrier, len(peers))


class Gather:
    def __init__(self, own, held, send, recv, hand_send, hand_recv):
        self.own, self.held = own, held
        self.send, self.recv = send, recv
        self.hand_send, self.hand_recv = hand_send, hand_recv
        self.x, self.y, self.z, self.core = place()
        self.dp = self.x * NY + self.y
        self.started = []

    def slot(self, z, core):
        return lax.rem(z + NZ, NZ) * 2 + core

    def part(self, z, core, step, way):
        view = self.held.at[self.slot(z, core)]
        if step < NZ // 2:
            return view
        return view.at[pl.ds(way * (ROWS // 2), ROWS // 2)]

    def hop(self, step, way):
        sign = 1 - 2 * way
        origin = self.z - sign * (step - 1)
        target = self.slot(self.z + sign, self.core)
        dst = self.part(origin, self.core, step, way)
        src = self.own if step == 1 and self.own is not None else dst
        return remote(
            src, dst, self.send.at[step - 1, way], self.recv.at[step - 1, way], self.dp, target
        )

    def hand(self, item, view, core):
        src = view if item or self.own is None else self.own
        return remote(
            src if core is None else view,
            view,
            self.hand_send.at[item],
            self.hand_recv.at[item],
            self.dp,
            self.slot(self.z, 1 - self.core),
        )

    def begin(self):
        for way in range(2):
            copy = self.hop(1, way)
            copy.start()
            self.started.append(copy)
        copy = self.hand(0, self.part(self.z, self.core, 1, 0), None)
        copy.start()
        self.started.append(copy)

    def advance(self, step):
        for way in range(2):
            sign = 1 - 2 * way
            view = self.part(self.z - sign * step, self.core, step, way)
            remote(
                view,
                view,
                self.send.at[step - 1, way],
                self.recv.at[step - 1, way],
                self.dp,
                self.slot(self.z + sign, self.core),
            ).wait_recv()
            if step < NZ // 2:
                copy = self.hop(step + 1, way)
                copy.start()
                self.started.append(copy)
            copy = self.hand(1 + 2 * (step - 1) + way, view, None)
            copy.start()
            self.started.append(copy)

    def finish(self):
        other = 1 - self.core
        self.hand(0, self.part(self.z, other, 1, 0), other).wait_recv()
        for step in range(1, NZ // 2 + 1):
            for way in range(2):
                sign = 1 - 2 * way
                view = self.part(self.z - sign * step, other, step, way)
                self.hand(1 + 2 * (step - 1) + way, view, other).wait_recv()
        for copy in self.started:
            copy.wait_send()


GATHER_SEMS = (
    pltpu.SemaphoreType.DMA((NZ // 2, 2)),
    pltpu.SemaphoreType.DMA((NZ // 2, 2)),
    pltpu.SemaphoreType.DMA((NZ + 1,)),
    pltpu.SemaphoreType.DMA((NZ + 1,)),
)


def collect_kernel(
    grad, factor, basis, all_grad, all_factor, all_basis,
    first_right, first_left, sum_right, sum_left,
    right_a, right_b, left_a, left_b, lane_sum, lane_in, half_out,
    own_sem,
    s1, r1, s2, r2, s3, r3, ys, yr, ex_send, ex_recv,
    *gather_sems,
):
    x, y, z, core = place()
    me = z * 2 + core
    side = lax.rem(y, 2)
    dp = x * NY + y
    right = lax.rem(x + 1, NX) * NY + y
    left = lax.rem(x + NX - 1, NX) * NY + y
    partner = x * NY + y + 1 - 2 * side
    peers = [(right, me), (left, me)]
    peers += [(x * NY + lax.rem(y + d, NY), me) for d in range(1, NY)]
    peers += [
        (dp, lax.rem(z + 1, NZ) * 2 + core),
        (dp, lax.rem(z + NZ - 1, NZ) * 2 + core),
        (dp, z * 2 + 1 - core),
    ]
    meet(peers)

    def region(owner, part, chunk):
        owner = lax.rem(owner + NX, NX)
        start = pl.multiple_of(lax.rem(owner, 2) * 4096 + part * 2048, 2048)
        return owner // 2, pl.ds(chunk * CROWS, CROWS), pl.ds(start, 2048)

    started = []

    def begin(copy):
        copy.start()
        started.append(copy)
        return copy

    for r in range(CHUNKS):
        begin(remote(grad.at[region(x + 2, 0, r)], first_right.at[r], s1.at[r, 0], r1.at[r, 0], right, me))
        begin(remote(grad.at[region(x - 2, 1, r)], first_left.at[r], s1.at[r, 1], r1.at[r, 1], left, me))
    own_basis = pltpu.make_async_copy(basis, all_basis.at[me], own_sem.at[0])
    own_factor = pltpu.make_async_copy(factor, all_factor.at[me], own_sem.at[1])
    own_basis.start()
    own_factor.start()
    gather_b = Gather(basis, all_basis, *gather_sems[0:4])
    gather_f = Gather(factor, all_factor, *gather_sems[4:8])
    gather_g = Gather(None, all_grad, *gather_sems[8:12])
    gather_b.begin()
    gather_f.begin()

    def forward(r):
        remote(first_right.at[r], first_right.at[r], s1.at[r, 0], r1.at[r, 0], right, me).wait_recv()
        own = grad[region(x + 1, 0, r)].astype(F32)
        sum_right[r] = (own + first_right[r].astype(F32)).astype(BF16)
        begin(remote(sum_right.at[r], right_a.at[r], s2.at[r, 0], r2.at[r, 0], right, me))
        begin(remote(grad.at[region(x + 1, 1, r)], right_b.at[r], s3.at[r, 0], r3.at[r, 0], right, me))
        remote(first_left.at[r], first_left.at[r], s1.at[r, 1], r1.at[r, 1], left, me).wait_recv()
        own = grad[region(x - 1, 1, r)].astype(F32)
        sum_left[r] = (own + first_left[r].astype(F32)).astype(BF16)
        begin(remote(sum_left.at[r], left_b.at[r], s2.at[r, 1], r2.at[r, 1], left, me))
        begin(remote(grad.at[region(x - 1, 0, r)], left_a.at[r], s3.at[r, 1], r3.at[r, 1], left, me))

    def turn(r):
        remote(right_a.at[r], right_a.at[r], s2.at[r, 0], r2.at[r, 0], right, me).wait_recv()
        remote(right_b.at[r], right_b.at[r], s3.at[r, 0], r3.at[r, 0], right, me).wait_recv()
        remote(left_b.at[r], left_b.at[r], s2.at[r, 1], r2.at[r, 1], left, me).wait_recv()
        remote(left_a.at[r], left_a.at[r], s3.at[r, 1], r3.at[r, 1], left, me).wait_recv()
        rows = pl.ds(r * CROWS, CROWS)
        for part, (from_left, from_right) in enumerate(((right_a, left_a), (right_b, left_b))):
            total = grad[region(x, part, r)].astype(F32)
            total = total + from_left[r].astype(F32) + from_right[r].astype(F32)
            total = total.astype(BF16)
            for piece in range(4):
                lane_sum[part * 4 + piece, rows] = total[:, piece * HALF:(piece + 1) * HALF]
        if r % 2:
            send_rows = pl.ds((r - 1) * CROWS, 2 * CROWS)
            for d in range(1, NY):
                target = lax.rem(y + d, NY)
                begin(remote(
                    lane_sum.at[target, send_rows], lane_in.at[d - 1, send_rows],
                    ys.at[d - 1, r // 2], yr.at[d - 1, r // 2], x * NY + target, me,
                ))

    mine = pl.ds(pl.multiple_of(side * HALF, HALF), HALF)
    theirs = pl.ds(pl.multiple_of((1 - side) * HALF, HALF), HALF)

    def land(h):
        rows = pl.ds(2 * h * CROWS, 2 * CROWS)
        total = lane_sum[y, rows].astype(F32)
        for d in range(1, NY):
            view = lane_in.at[d - 1, rows]
            remote(view, view, ys.at[d - 1, h], yr.at[d - 1, h], x * NY + lax.rem(y + d, NY), me).wait_recv()
        for d in range(1, NY):
            total = total + lane_in[d - 1, rows].astype(F32)
        total = total.astype(BF16)
        half_out[rows] = total
        all_grad[me, rows, mine] = total
        begin(remote(half_out.at[rows], all_grad.at[me, rows, mine], ex_send.at[h], ex_recv.at[h], partner, me))

    forward(0)
    forward(1)
    forward(2)
    gather_b.advance(1)
    forward(3)
    gather_f.advance(1)
    turn(0)
    turn(1)
    gather_b.advance(2)
    turn(2)
    gather_f.advance(2)
    turn(3)
    land(0)
    land(1)
    gather_b.advance(3)
    for h in range(2):
        view = all_grad.at[me, pl.ds(2 * h * CROWS, 2 * CROWS), theirs]
        remote(view, view, ex_send.at[h], ex_recv.at[h], partner, me).wait_recv()
    gather_g.begin()
    gather_f.advance(3)
    gather_g.advance(1)
    gather_b.advance(4)
    gather_f.advance(4)
    gather_g.advance(2)
    gather_g.advance(3)
    gather_g.advance(4)
    own_basis.wait()
    own_factor.wait()
    gather_b.finish()
    gather_f.finish()
    gather_g.finish()
    for copy in started:
        copy.wait_send()


def collect(grad, factor, basis):
    slots = 2 * NZ
    chunk = pltpu.VMEM((CHUNKS, CROWS, 2048), BF16)
    dma = pltpu.SemaphoreType.DMA
    return pl.pallas_call(
        collect_kernel,
        out_shape=(
            jax.ShapeDtypeStruct((slots, ROWS, BLOCK), BF16),
            jax.ShapeDtypeStruct((slots, ROWS, BLOCK), BF16),
            jax.ShapeDtypeStruct((slots, ROWS, BLOCK), F32),
        ),
        in_specs=[VMEM_SPEC] * 3,
        out_specs=(VMEM_SPEC,) * 3,
        scratch_shapes=[chunk] * 8
        + [
            pltpu.VMEM((NY, ROWS, HALF), BF16),
            pltpu.VMEM((NY - 1, ROWS, HALF), BF16),
            pltpu.VMEM((ROWS, HALF), BF16),
            dma((2,)),
        ]
        + [dma((CHUNKS, 2))] * 6
        + [dma((NY - 1, 2))] * 2
        + [dma((2,))] * 2
        + list(GATHER_SEMS) * 3,
        compiler_params=pltpu.CompilerParams(
            collective_id=0, has_side_effects=True, vmem_limit_bytes=VMEM_BYTES
        ),
        name="collect",
    )(grad, factor, basis)


def split(value):
    high = value.astype(BF16)
    return high, (value - high.astype(F32)).astype(BF16)


def dot3(left, right, numbers):
    dot = functools.partial(lax.dot_general, dimension_numbers=numbers, preferred_element_type=F32)
    return dot(left[0], right[0]) + (dot(left[0], right[1]) + dot(left[1], right[0]))


def factor_inverse(rows):
    count = len(rows)
    shape = rows[0].shape
    lane = lax.broadcasted_iota(jnp.int32, shape, 1)
    sub = lax.broadcasted_iota(jnp.int32, shape, 0)
    rows = list(rows)
    done = []
    for group in range(count):
        base = 8 * group
        pivot_rows = rows[group]
        columns = [jnp.broadcast_to(pivot_rows[:, base + l:base + l + 1], shape) for l in range(8)]
        result = jnp.zeros(shape, F32)
        for k in range(8):
            own = sub == k
            pivot = jnp.broadcast_to(columns[k][k:k + 1], shape)
            inverse = 1.0 / pivot
            row = jnp.where(lane == base + k, 1.0, jnp.broadcast_to(pivot_rows[k:k + 1], shape))
            result = jnp.where(own, row * lax.rsqrt(pivot), result)
            scale = jnp.where(own, -inverse, columns[k] * inverse)
            pivot_rows = jnp.where(own | (lane == base + k), 0.0, pivot_rows) - scale * row
            for l in range(k + 1, 8):
                columns[l] = jnp.where(own, 0.0, columns[l]) - scale * jnp.broadcast_to(
                    columns[l][k:k + 1], shape
                )
        done.append(jnp.where(lane <= base + sub, result, 0.0))
        if group + 1 < count:
            spread = [jnp.broadcast_to(pivot_rows[l:l + 1], shape) for l in range(8)]
            inside = (lane >= base) & (lane < base + 8)
            for n in range(group + 1, count):
                total = jnp.where(inside, 0.0, rows[n])
                for l in range(8):
                    total = total - jnp.broadcast_to(rows[n][:, base + l:base + l + 1], shape) * spread[l]
                rows[n] = total
    return done


def refresh_kernel(
    grad, factor, basis, own_factor, new_factor, basis_t, new_rows,
    power, high, low, gram, inverse,
):
    x, y, z, core = place()
    me = z * 2 + core
    side = lax.rem(y, 2)
    tile = 256

    @pl.when(side == 0)
    def _():
        @pl.loop(0, BLOCK // tile)
        def _(i):
            rows = pl.ds(pl.multiple_of(i * tile, tile), tile)
            power[rows, :] = lax.dot_general(grad[rows, :], grad[...], NT, preferred_element_type=F32)

    @pl.when(side == 1)
    def _():
        @pl.loop(0, BLOCK // tile)
        def _(i):
            rows = pl.ds(pl.multiple_of(i * tile, tile), tile)
            power[rows, :] = lax.dot_general(grad[:, rows], grad[...], TN, preferred_element_type=F32)

    mine = pl.ds(pl.multiple_of(me * ROWS, ROWS), ROWS)
    new_factor[...] = 0.95 * own_factor[...] + 0.05 * power[mine, :]

    @pl.loop(0, BLOCK // PANEL)
    def _(i):
        rows = pl.ds(pl.multiple_of(i * PANEL, PANEL), PANEL)
        now = 0.95 * factor[rows, :].astype(F32) + 0.05 * power[rows, :]
        high[rows, :], low[rows, :] = split(now)

    @pl.loop(0, BLOCK // tile)
    def _(i):
        rows = pl.ds(pl.multiple_of(i * tile, tile), tile)
        power[rows, :] = dot3(split(basis[:, rows]), (high[...], low[...]), TN)

    @pl.loop(0, BLOCK // PANEL)
    def _(k):
        rows = pl.ds(pl.multiple_of(k * PANEL, PANEL), PANEL)
        panel = split(power[rows, :])
        gram[...] = dot3(panel, panel, NT)
        done = factor_inverse([gram[8 * i:8 * i + 8, :] for i in range(PANEL // 8)])
        for i in range(PANEL // 8):
            inverse[8 * i:8 * i + 8, :] = done[i]
        fresh = dot3(split(inverse[...]), panel, NN)
        basis_t[rows, :] = fresh.astype(BF16)
        fresh = split(fresh)

        @pl.loop(k + 1, BLOCK // PANEL)
        def _(j):
            later = pl.ds(pl.multiple_of(j * PANEL, PANEL), PANEL)
            old = power[later, :]
            overlap = dot3(split(old), fresh, NT)
            power[later, :] = old - dot3(split(overlap), fresh, NN)

    pick = lax.broadcasted_iota(jnp.int32, (ROWS, BLOCK), 1) == me * ROWS + lax.broadcasted_iota(
        jnp.int32, (ROWS, BLOCK), 0
    )
    new_rows[...] = lax.dot_general(
        pick.astype(BF16), basis_t[...], NT, preferred_element_type=F32
    ).astype(BF16)


def refresh(grad, factor, basis, own_factor):
    return pl.pallas_call(
        refresh_kernel,
        out_shape=(
            jax.ShapeDtypeStruct((ROWS, BLOCK), F32),
            jax.ShapeDtypeStruct((BLOCK, BLOCK), BF16),
            jax.ShapeDtypeStruct((ROWS, BLOCK), BF16),
        ),
        in_specs=[VMEM_SPEC] * 4,
        out_specs=(VMEM_SPEC,) * 3,
        scratch_shapes=[
            pltpu.VMEM((BLOCK, BLOCK), F32),
            pltpu.VMEM((BLOCK, BLOCK), BF16),
            pltpu.VMEM((BLOCK, BLOCK), BF16),
            pltpu.VMEM((PANEL, PANEL), F32),
            pltpu.VMEM((PANEL, PANEL), F32),
        ],
        compiler_params=pltpu.CompilerParams(vmem_limit_bytes=VMEM_BYTES),
        name="refresh",
    )(grad, factor, basis, own_factor)


def rotate_kernel(
    basis_t, grad, new_rows, first, second, new_first, new_second, direction,
    mixed, mixed_in, left_rows, part, part_in, normal, all_normal, weighted, weighted_in, turned, turned_in,
    send, recv, *gather_sems,
):
    x, y, z, core = place()
    me = z * 2 + core
    side = lax.rem(y, 2)
    dp = x * NY + y
    partner = dp + 1 - 2 * side
    meet([
        (partner, me),
        (dp, lax.rem(z + 1, NZ) * 2 + core),
        (dp, lax.rem(z + NZ - 1, NZ) * 2 + core),
        (dp, z * 2 + 1 - core),
    ])

    def across(src, dst, i):
        return remote(src, dst, send.at[i], recv.at[i], partner, me)

    def dot(a, b, numbers):
        return lax.dot_general(a, b, numbers, preferred_element_type=F32)

    to_mixed = across(mixed, mixed_in, 0)
    to_rows = across(new_rows, left_rows, 1)
    to_part = across(part, part_in, 2)
    to_weighted = across(weighted, weighted_in, 3)
    to_turned = across(turned, turned_in, 4)
    gather = Gather(normal, all_normal, *gather_sems)
    mine = pl.ds(pl.multiple_of(me * ROWS, ROWS), ROWS)

    @pl.when(side == 0)
    def _():
        mixed[...] = dot(basis_t[mine, :], grad[...], NN).astype(BF16)
        to_mixed.start()
        to_rows.start()
        to_part.wait_recv()

    @pl.when(side == 1)
    def _():
        to_mixed.wait_recv()
        part[...] = dot(mixed_in[...], basis_t[0:HALF, :], NT)
        to_part.start()
        part_in[...] = dot(mixed_in[...], basis_t[HALF:BLOCK, :], NT)

    rotated = part_in[...]
    first_now = 0.95 * first[...] + 0.05 * rotated
    second_now = 0.95 * second[...] + 0.05 * rotated * rotated
    now = (first_now / (jnp.sqrt(second_now) + 1e-08)).astype(BF16)
    normal[...] = now
    all_normal[me] = now
    gather.begin()
    new_first[...] = first_now
    new_second[...] = second_now

    @pl.when(side == 0)
    def _():
        left_rows[...] = new_rows[...]

    @pl.when(side == 1)
    def _():
        to_rows.wait_recv()

    gather.advance(1)
    gather.advance(2)
    gather.advance(3)
    gather.advance(4)
    gather.finish()
    weighted[...] = dot(left_rows[...], all_normal[...].reshape(BLOCK, HALF), NN).astype(BF16)

    @pl.when(side == 0)
    def _():
        to_weighted.start()
        to_turned.wait_recv()
        direction[...] = turned_in[...]
        to_mixed.wait_send()
        to_rows.wait_send()
        to_weighted.wait_send()

    @pl.when(side == 1)
    def _():
        own = dot(weighted[...], basis_t[HALF:BLOCK, :], NN)
        to_weighted.wait_recv()
        total = (own + dot(weighted_in[...], basis_t[0:HALF, :], NN)).astype(BF16)
        turned[...] = total[:, 0:HALF]
        to_turned.start()
        direction[...] = total[:, HALF:BLOCK]
        to_part.wait_send()
        to_turned.wait_send()


def rotate(basis_t, grad, new_rows, first, second):
    dma = pltpu.SemaphoreType.DMA
    return pl.pallas_call(
        rotate_kernel,
        out_shape=(
            jax.ShapeDtypeStruct((ROWS, HALF), F32),
            jax.ShapeDtypeStruct((ROWS, HALF), F32),
            jax.ShapeDtypeStruct((ROWS, HALF), BF16),
        ),
        in_specs=[VMEM_SPEC] * 5,
        out_specs=(VMEM_SPEC,) * 3,
        scratch_shapes=[
            pltpu.VMEM((ROWS, BLOCK), BF16),
            pltpu.VMEM((ROWS, BLOCK), BF16),
            pltpu.VMEM((ROWS, BLOCK), BF16),
            pltpu.VMEM((ROWS, HALF), F32),
            pltpu.VMEM((ROWS, HALF), F32),
            pltpu.VMEM((ROWS, HALF), BF16),
            pltpu.VMEM((2 * NZ, ROWS, HALF), BF16),
            pltpu.VMEM((ROWS, HALF), BF16),
            pltpu.VMEM((ROWS, HALF), BF16),
            pltpu.VMEM((ROWS, HALF), BF16),
            pltpu.VMEM((ROWS, HALF), BF16),
            dma((5,)),
            dma((5,)),
            *GATHER_SEMS,
        ],
        compiler_params=pltpu.CompilerParams(
            collective_id=1, has_side_effects=True, vmem_limit_bytes=VMEM_BYTES
        ),
        name="rotate",
    )(basis_t, grad, new_rows, first, second)


def body(grad_partial, factors, bases, first_moment, second_moment):
    all_grad, all_factor, all_basis = collect(grad_partial[0], factors[0].astype(BF16), bases[0])
    whole = (BLOCK, BLOCK)
    all_grad = all_grad.reshape(whole)
    new_factor, basis_t, new_rows = refresh(
        all_grad, all_factor.reshape(whole), all_basis.reshape(whole), factors[0]
    )
    first_new, second_new, direction = rotate(
        basis_t, all_grad, new_rows, first_moment[0], second_moment[0]
    )
    return (new_factor[None], new_rows[None], first_new[None], second_new[None], direction[None])


def solution(mesh):
    spec = P("dp", "fsdp", None)
    return jax.shard_map(
        body,
        mesh=mesh,
        in_specs=(P("dp", None, "fsdp", None), spec, spec, spec, spec),
        out_specs=(spec,) * 5,
        check_vma=False,
    )
```

time: 973 us -> 207 us (0.21)
  waiting for transfers between devices: 576 us -> 0 us
  other arithmetic: 265 us -> 1.62 us
  Pallas kernels: 0 us -> 200 us
  matrix products: 53.3 us -> 0 us
  local copies, waits for them, and re-layouts: 44.1 us -> 4.61 us
  between operations: 19.8 us -> 0.65 us
    another operation x33 -> x0, other arithmetic: 257 us -> none  [the longest x30 173 us: body(): cholesky_factor = jnp.linalg.cholesky(gram_matrix)]
    reduce_scatter x1 -> x0, waiting for transfers between devices: 224 us -> none  [body(): lax.psum_scatter(summand.astype(jnp.bfloat16), 'dp', scatter_dimension=0,...]
    all_gather x5 -> x0, waiting for transfers between devices: 218 us -> none  [the longest x1 47.6 us: body(): whole_block = lax.all_gather(own_rows, 'fsdp', axis=0, tiled=True)]
    pallas_call x0 -> x3, Pallas kernels: none -> 200 us  [the longest x1 91.6 us: refresh(): pl.pallas_call(refresh_kernel, out_shape=(jax.ShapeDtypeStruct((ROWS, BLO...]
    psum x1 -> x0, waiting for transfers between devices: 125 us -> none  [body(): lax.psum(jnp.dot(power_rows.T, power_rows, precision=lax.Precision.HIGHES...]
    another operation x37 -> x0, local copies, waits for them, and re-layouts: 36.5 us -> none
    another operation x29 -> x0, matrix products: 34.3 us -> none  [the longest x14 23.2 us: body(): cholesky_factor = jnp.linalg.cholesky(gram_matrix)]
    dot_general x6 -> x0, matrix products: 19 us -> none  [the longest x1 5.06 us: body(): jnp.dot(power_rows.T, power_rows, precision=lax.Precision.HIGHEST, prefer...]
  transfers between devices with their start and end apart: 10 -> 0, of which waited for: 10 -> 0; matrix products, arithmetic and copies ran while one was open for 0% -> 0% of each run, Pallas kernels for 0% -> 0%
where the time goes in v1:
time: 207 us; the launch traced here: 206 us
  Pallas kernels  200 us (97%)
  local copies, waits for them, and re-layouts  4.61 us (2%)
    pallas_call x1, Pallas kernels, refresh(): pl.pallas_call(refresh_kernel, out_shape=(jax.ShapeDtypeStruct((ROWS, BLO...  91.6 us
    pallas_call x1, Pallas kernels, collect(): pl.pallas_call(collect_kernel, out_shape=(jax.ShapeDtypeStruct((slots, RO...  71 us
    pallas_call x1, Pallas kernels, rotate(): pl.pallas_call(rotate_kernel, out_shape=(jax.ShapeDtypeStruct((ROWS, HALF...  36.9 us
    unnamed x3, local copies, waits for them, and re-layouts  4.61 us

profile of v1, /device:TPU:1, one launch (start us, length us, event | category | flops | bytes accessed | tf_op | source)
XLA Modules:
  0.0 206.4 jit_solution(12350276537203402317)
XLA Ops:
  0.6 1.6 bitcast_convert_fusion.factor
  2.3 71.0 %collect.1 = (bf16[16,64,1024]{2,1,0:T(8,128)(2,1)}, bf16[16,64,1024]{2,1,0:T(8,128)(2,1)}, f32[16,64,1024]{2,1,0:T(8,128)}) custom-call(bf16[2,64,8192]{2,1,0:T(8,128)(2,1)} %bitcast.17, bf16[64,1024]{1,0:T(8,128)(2,1)} %bitcast_convert_fusion.factor, f32[64,1024]{1,0:T(8,128)} %bitcast.20), custom_call_target="tpu_custom_call" | custom-call | tf_op jit(solution)/shard_map/collect/pallas_call | solution.py:280
  73.3 91.6 %refresh.1 = (f32[64,1024]{1,0:T(8,128)}, bf16[1024,1024]{1,0:T(8,128)(2,1)}, bf16[64,1024]{1,0:T(8,128)(2,1)}) custom-call(bf16[1024,1024]{1,0:T(8,128)(2,1)} %bitcast.14, bf16[1024,1024]{1,0:T(8,128)(2,1)} %bitcast.18, f32[1024,1024]{1,0:T(8,128)} %bitcast.16, f32[64,1024]{1,0:T(8,128)} %bitcast.19), custom_call_target="tpu_custom_call" | custom-call | tf_op jit(solution)/shard_map/refresh/pallas_call | solution.py:418
  164.8 36.9 %rotate.1 = (f32[64,512]{1,0:T(8,128)}, f32[64,512]{1,0:T(8,128)}, bf16[64,512]{1,0:T(8,128)(2,1)}) custom-call(bf16[1024,1024]{1,0:T(8,128)(2,1)} %get-tuple-element.19.basis_t, bf16[1024,1024]{1,0:T(8,128)(2,1)} %bitcast.15, bf16[64,1024]{1,0:T(8,128)(2,1)} %get-tuple-element.18.new_rows, f32[64,512]{1,0:T(8,128)} %bitcast.21, f32[64,512]{1,0:T(8,128)} %bitcast.22), custom_call_target="tpu_custom_call" | custom-call | tf_op jit(solution)/shard_map/rotate/pallas_call | solution.py:532
  201.8 1.6 copy.13
  203.3 1.6 copy.14
  204.9 1.5 copy.15

commit v2 on v1

--- a/solution.py
+++ b/solution.py
@@ -20,7 +20,7 @@
 CROWS = ROWS // CHUNKS
 PANEL = 128
 VMEM_SPEC = pl.BlockSpec(memory_space=pltpu.VMEM)
-VMEM_BYTES = 60 << 20
+VMEM_BYTES = 40 << 20
 
 
 def place():
@@ -53,8 +53,9 @@
 
 
 class Gather:
-    def __init__(self, own, held, send, recv, hand_send, hand_recv):
+    def __init__(self, own, held, send, recv, hand_send, hand_recv, start=0, count=ROWS):
         self.own, self.held = own, held
+        self.start, self.count = start, count
         self.send, self.recv = send, recv
         self.hand_send, self.hand_recv = hand_send, hand_recv
         self.x, self.y, self.z, self.core = place()
@@ -65,10 +66,11 @@
         return lax.rem(z + NZ, NZ) * 2 + core
 
     def part(self, z, core, step, way):
-        view = self.held.at[self.slot(z, core)]
-        if step < NZ // 2:
-            return view
-        return view.at[pl.ds(way * (ROWS // 2), ROWS // 2)]
+        start, count = self.start, self.count
+        if step == NZ // 2:
+            count = count // 2
+            start = start + way * count
+        return self.held.at[self.slot(z, core), pl.ds(start, count)]
 
     def hop(self, step, way):
         sign = 1 - 2 * way
@@ -179,13 +181,14 @@
     for r in range(CHUNKS):
         begin(remote(grad.at[region(x + 2, 0, r)], first_right.at[r], s1.at[r, 0], r1.at[r, 0], right, me))
         begin(remote(grad.at[region(x - 2, 1, r)], first_left.at[r], s1.at[r, 1], r1.at[r, 1], left, me))
-    own_basis = pltpu.make_async_copy(basis, all_basis.at[me], own_sem.at[0])
-    own_factor = pltpu.make_async_copy(factor, all_factor.at[me], own_sem.at[1])
+    own_basis = pltpu.make_async_copy(basis, all_basis.at[me], own_sem)
     own_basis.start()
-    own_factor.start()
+    all_factor[me] = factor[...].astype(BF16)
     gather_b = Gather(basis, all_basis, *gather_sems[0:4])
-    gather_f = Gather(factor, all_factor, *gather_sems[4:8])
-    gather_g = Gather(None, all_grad, *gather_sems[8:12])
+    gather_f = Gather(None, all_factor, *gather_sems[4:8])
+    gather_g = [
+        Gather(None, all_grad, *gather_sems[8 + 4 * h:12 + 4 * h], 2 * h * CROWS, 2 * CROWS) for h in range(2)
+    ]
     gather_b.begin()
     gather_f.begin()
 
@@ -238,37 +241,44 @@
         all_grad[me, rows, mine] = total
         begin(remote(half_out.at[rows], all_grad.at[me, rows, mine], ex_send.at[h], ex_recv.at[h], partner, me))
 
+    def paired(h):
+        view = all_grad.at[me, pl.ds(2 * h * CROWS, 2 * CROWS), theirs]
+        remote(view, view, ex_send.at[h], ex_recv.at[h], partner, me).wait_recv()
+        gather_g[h].begin()
+
     forward(0)
     forward(1)
     forward(2)
     gather_b.advance(1)
     forward(3)
+    turn(0)
     gather_f.advance(1)
-    turn(0)
     turn(1)
+    turn(2)
     gather_b.advance(2)
-    turn(2)
+    turn(3)
     gather_f.advance(2)
-    turn(3)
     land(0)
+    gather_b.advance(3)
+    paired(0)
     land(1)
-    gather_b.advance(3)
-    for h in range(2):
-        view = all_grad.at[me, pl.ds(2 * h * CROWS, 2 * CROWS), theirs]
-        remote(view, view, ex_send.at[h], ex_recv.at[h], partner, me).wait_recv()
-    gather_g.begin()
+    gather_g[0].advance(1)
+    paired(1)
     gather_f.advance(3)
-    gather_g.advance(1)
+    gather_g[0].advance(2)
+    gather_g[1].advance(1)
     gather_b.advance(4)
     gather_f.advance(4)
-    gather_g.advance(2)
-    gather_g.advance(3)
-    gather_g.advance(4)
+    gather_g[0].advance(3)
+    gather_g[1].advance(2)
+    gather_g[0].advance(4)
+    gather_g[1].advance(3)
+    gather_g[1].advance(4)
     own_basis.wait()
-    own_factor.wait()
     gather_b.finish()
     gather_f.finish()
-    gather_g.finish()
+    gather_g[0].finish()
+    gather_g[1].finish()
     for copy in started:
         copy.wait_send()
 
@@ -291,12 +301,12 @@
             pltpu.VMEM((NY, ROWS, HALF), BF16),
             pltpu.VMEM((NY - 1, ROWS, HALF), BF16),
             pltpu.VMEM((ROWS, HALF), BF16),
-            dma((2,)),
+            dma(()),
         ]
         + [dma((CHUNKS, 2))] * 6
         + [dma((NY - 1, 2))] * 2
         + [dma((2,))] * 2
-        + list(GATHER_SEMS) * 3,
+        + list(GATHER_SEMS) * 4,
         compiler_params=pltpu.CompilerParams(
             collective_id=0, has_side_effects=True, vmem_limit_bytes=VMEM_BYTES
         ),
@@ -319,40 +329,61 @@
     shape = rows[0].shape
     lane = lax.broadcasted_iota(jnp.int32, shape, 1)
     sub = lax.broadcasted_iota(jnp.int32, shape, 0)
+
+    def along(value, column):
+        return jnp.broadcast_to(value[:, column:column + 1], shape)
+
+    def down(value, row):
+        return jnp.broadcast_to(value[row:row + 1], shape)
+
     rows = list(rows)
     done = []
+    columns = [along(rows[0], l) for l in range(8)]
     for group in range(count):
         base = 8 * group
-        pivot_rows = rows[group]
-        columns = [jnp.broadcast_to(pivot_rows[:, base + l:base + l + 1], shape) for l in range(8)]
+        here = rows[group]
+        more = group + 1 < count
         result = jnp.zeros(shape, F32)
+        if more:
+            below = rows[group + 1]
+            below_columns = [along(below, base + l) for l in range(8)]
+            next_columns = [along(below, base + 8 + l) for l in range(8)]
         for k in range(8):
             own = sub == k
-            pivot = jnp.broadcast_to(columns[k][k:k + 1], shape)
+            pivot = down(columns[k], k)
             inverse = 1.0 / pivot
-            row = jnp.where(lane == base + k, 1.0, jnp.broadcast_to(pivot_rows[k:k + 1], shape))
+            row = jnp.where(lane == base + k, 1.0, down(here, k))
+            ahead = [down(columns[l], k) for l in range(k + 1, 8)]
             result = jnp.where(own, row * lax.rsqrt(pivot), result)
             scale = jnp.where(own, -inverse, columns[k] * inverse)
-            pivot_rows = jnp.where(own | (lane == base + k), 0.0, pivot_rows) - scale * row
+            here = jnp.where(own | (lane == base + k), 0.0, here) - scale * row
             for l in range(k + 1, 8):
-                columns[l] = jnp.where(own, 0.0, columns[l]) - scale * jnp.broadcast_to(
-                    columns[l][k:k + 1], shape
-                )
+                columns[l] = jnp.where(own, 0.0, columns[l]) - scale * ahead[l - k - 1]
+            if more:
+                scale = below_columns[k] * inverse
+                below = jnp.where(lane == base + k, 0.0, below) - scale * row
+                for l in range(k + 1, 8):
+                    below_columns[l] = below_columns[l] - scale * ahead[l - k - 1]
+                for l in range(8):
+                    next_columns[l] = next_columns[l] - scale * down(below_columns[k], l)
         done.append(jnp.where(lane <= base + sub, result, 0.0))
-        if group + 1 < count:
-            spread = [jnp.broadcast_to(pivot_rows[l:l + 1], shape) for l in range(8)]
+        if more:
+            rows[group + 1] = below
+            columns = next_columns
+        if group + 2 < count:
+            spread = [down(here, l) for l in range(8)]
             inside = (lane >= base) & (lane < base + 8)
-            for n in range(group + 1, count):
-                total = jnp.where(inside, 0.0, rows[n])
-                for l in range(8):
-                    total = total - jnp.broadcast_to(rows[n][:, base + l:base + l + 1], shape) * spread[l]
-                rows[n] = total
+            for n in range(group + 2, count):
+                terms = [along(rows[n], base + l) * spread[l] for l in range(8)]
+                while len(terms) > 1:
+                    terms = [terms[i] + terms[i + 1] for i in range(0, len(terms), 2)]
+                rows[n] = jnp.where(inside, 0.0, rows[n]) - terms[0]
     return done
 
 
 def refresh_kernel(
     grad, factor, basis, own_factor, new_factor, basis_t, new_rows,
-    power, high, low, gram, inverse,
+    power, high, low, gram, upper, lower,
 ):
     x, y, z, core = place()
     me = z * 2 + core
@@ -387,21 +418,35 @@
         rows = pl.ds(pl.multiple_of(i * tile, tile), tile)
         power[rows, :] = dot3(split(basis[:, rows]), (high[...], low[...]), TN)
 
-    @pl.loop(0, BLOCK // PANEL)
+    def factored(dst, corner):
+        rows = [gram[corner + 8 * i:corner + 8 * i + 8, corner:corner + PANEL] for i in range(PANEL // 8)]
+        for i, value in enumerate(factor_inverse(rows)):
+            dst[8 * i:8 * i + 8, :] = value
+        return split(dst[...])
+
+    top, bottom = slice(0, PANEL), slice(PANEL, 2 * PANEL)
+
+    @pl.loop(0, BLOCK // tile)
     def _(k):
-        rows = pl.ds(pl.multiple_of(k * PANEL, PANEL), PANEL)
+        rows = pl.ds(pl.multiple_of(k * tile, tile), tile)
         panel = split(power[rows, :])
         gram[...] = dot3(panel, panel, NT)
-        done = factor_inverse([gram[8 * i:8 * i + 8, :] for i in range(PANEL // 8)])
-        for i in range(PANEL // 8):
-            inverse[8 * i:8 * i + 8, :] = done[i]
-        fresh = dot3(split(inverse[...]), panel, NN)
+        first = factored(upper, 0)
+        below = split(dot3(split(gram[bottom, top]), first, NT))
+        gram[bottom, bottom] = gram[bottom, bottom] - dot3(below, below, NT)
+        cross = split(dot3(below, first, NN))
+        second = factored(lower, PANEL)
+        gram[top, top] = upper[...]
+        gram[top, bottom] = jnp.zeros((PANEL, PANEL), F32)
+        gram[bottom, top] = -dot3(second, cross, NN)
+        gram[bottom, bottom] = lower[...]
+        fresh = dot3(split(gram[...]), panel, NN)
         basis_t[rows, :] = fresh.astype(BF16)
         fresh = split(fresh)
 
-        @pl.loop(k + 1, BLOCK // PANEL)
+        @pl.loop(k + 1, BLOCK // tile)
         def _(j):
-            later = pl.ds(pl.multiple_of(j * PANEL, PANEL), PANEL)
+            later = pl.ds(pl.multiple_of(j * tile, tile), tile)
             old = power[later, :]
             overlap = dot3(split(old), fresh, NT)
             power[later, :] = old - dot3(split(overlap), fresh, NN)
@@ -428,6 +473,7 @@
             pltpu.VMEM((BLOCK, BLOCK), F32),
             pltpu.VMEM((BLOCK, BLOCK), BF16),
             pltpu.VMEM((BLOCK, BLOCK), BF16),
+            pltpu.VMEM((2 * PANEL, 2 * PANEL), F32),
             pltpu.VMEM((PANEL, PANEL), F32),
             pltpu.VMEM((PANEL, PANEL), F32),
         ],
@@ -438,7 +484,7 @@
 
 def rotate_kernel(
     basis_t, grad, new_rows, first, second, new_first, new_second, direction,
-    mixed, mixed_in, left_rows, part, part_in, normal, all_normal, weighted, weighted_in, turned, turned_in,
+    mixed, mixed_in, left_rows, part, part_in, all_normal, weighted, weighted_in, turned, turned_in,
     send, recv, *gather_sems,
 ):
     x, y, z, core = place()
@@ -459,72 +505,80 @@
     def dot(a, b, numbers):
         return lax.dot_general(a, b, numbers, preferred_element_type=F32)
 
-    to_mixed = across(mixed, mixed_in, 0)
-    to_rows = across(new_rows, left_rows, 1)
-    to_part = across(part, part_in, 2)
-    to_weighted = across(weighted, weighted_in, 3)
-    to_turned = across(turned, turned_in, 4)
-    gather = Gather(normal, all_normal, *gather_sems)
+    count = ROWS // 2
+    halves = [pl.ds(h * count, count) for h in range(2)]
+    to_rows = across(new_rows, left_rows, 0)
+    to_mixed = [across(mixed.at[r], mixed_in.at[r], 1 + h) for h, r in enumerate(halves)]
+    to_part = [across(part.at[r], part_in.at[r], 3 + h) for h, r in enumerate(halves)]
+    to_weighted = [across(weighted.at[r], weighted_in.at[r], 5 + h) for h, r in enumerate(halves)]
+    to_turned = [across(turned.at[r], turned_in.at[r], 7 + h) for h, r in enumerate(halves)]
+    gathers = [
+        Gather(None, all_normal, *gather_sems[4 * h:4 * h + 4], h * count, count) for h in range(2)
+    ]
     mine = pl.ds(pl.multiple_of(me * ROWS, ROWS), ROWS)
 
     @pl.when(side == 0)
     def _():
         mixed[...] = dot(basis_t[mine, :], grad[...], NN).astype(BF16)
-        to_mixed.start()
+        for copy in to_mixed:
+            copy.start()
         to_rows.start()
-        to_part.wait_recv()
-
-    @pl.when(side == 1)
-    def _():
-        to_mixed.wait_recv()
-        part[...] = dot(mixed_in[...], basis_t[0:HALF, :], NT)
-        to_part.start()
-        part_in[...] = dot(mixed_in[...], basis_t[HALF:BLOCK, :], NT)
-
-    rotated = part_in[...]
-    first_now = 0.95 * first[...] + 0.05 * rotated
-    second_now = 0.95 * second[...] + 0.05 * rotated * rotated
-    now = (first_now / (jnp.sqrt(second_now) + 1e-08)).astype(BF16)
-    normal[...] = now
-    all_normal[me] = now
-    gather.begin()
-    new_first[...] = first_now
-    new_second[...] = second_now
-
-    @pl.when(side == 0)
-    def _():
         left_rows[...] = new_rows[...]
+
+    for h, rows in enumerate(halves):
+        @pl.when(side == 0)
+        def _():
+            to_part[h].wait_recv()
+
+        @pl.when(side == 1)
+        def _():
+            to_mixed[h].wait_recv()
+            now = mixed_in[rows, :]
+            part[rows, :] = dot(now, basis_t[0:HALF, :], NT)
+            to_part[h].start()
+            part_in[rows, :] = dot(now, basis_t[HALF:BLOCK, :], NT)
+
+        rotated = part_in[rows, :]
+        first_now = 0.95 * first[rows, :] + 0.05 * rotated
+        second_now = 0.95 * second[rows, :] + 0.05 * rotated * rotated
+        all_normal[me, rows] = (first_now / (jnp.sqrt(second_now) + 1e-08)).astype(BF16)
+        gathers[h].begin()
+        new_first[rows, :] = first_now
+        new_second[rows, :] = second_now
 
     @pl.when(side == 1)
     def _():
         to_rows.wait_recv()
 
-    gather.advance(1)
-    gather.advance(2)
-    gather.advance(3)
-    gather.advance(4)
-    gather.finish()
+    for step in range(1, NZ // 2 + 1):
+        for gather in gathers:
+            gather.advance(step)
+    for gather in gathers:
+        gather.finish()
     weighted[...] = dot(left_rows[...], all_normal[...].reshape(BLOCK, HALF), NN).astype(BF16)
 
     @pl.when(side == 0)
     def _():
-        to_weighted.start()
-        to_turned.wait_recv()
-        direction[...] = turned_in[...]
-        to_mixed.wait_send()
-        to_rows.wait_send()
-        to_weighted.wait_send()
+        for copy in to_weighted:
+            copy.start()
+        for h, rows in enumerate(halves):
+            to_turned[h].wait_recv()
+            direction[rows, :] = turned_in[rows, :]
+        for copy in [to_rows] + to_mixed + to_weighted:
+            copy.wait_send()
 
     @pl.when(side == 1)
     def _():
         own = dot(weighted[...], basis_t[HALF:BLOCK, :], NN)
-        to_weighted.wait_recv()
-        total = (own + dot(weighted_in[...], basis_t[0:HALF, :], NN)).astype(BF16)
-        turned[...] = total[:, 0:HALF]
-        to_turned.start()
-        direction[...] = total[:, HALF:BLOCK]
-        to_part.wait_send()
-        to_turned.wait_send()
+        for h, rows in enumerate(halves):
+            to_weighted[h].wait_recv()
+            total = own[h * count:(h + 1) * count] + dot(weighted_in[rows, :], basis_t[0:HALF, :], NN)
+            total = total.astype(BF16)
+            turned[rows, :] = total[:, 0:HALF]
+            to_turned[h].start()
+            direction[rows, :] = total[:, HALF:BLOCK]
+        for copy in to_part + to_turned:
+            copy.wait_send()
 
 
 def rotate(basis_t, grad, new_rows, first, second):
@@ -544,14 +598,14 @@
             pltpu.VMEM((ROWS, BLOCK), BF16),
             pltpu.VMEM((ROWS, HALF), F32),
             pltpu.VMEM((ROWS, HALF), F32),
-            pltpu.VMEM((ROWS, HALF), BF16),
             pltpu.VMEM((2 * NZ, ROWS, HALF), BF16),
             pltpu.VMEM((ROWS, HALF), BF16),
             pltpu.VMEM((ROWS, HALF), BF16),
             pltpu.VMEM((ROWS, HALF), BF16),
             pltpu.VMEM((ROWS, HALF), BF16),
-            dma((5,)),
-            dma((5,)),
+            dma((9,)),
+            dma((9,)),
+            *GATHER_SEMS,
             *GATHER_SEMS,
         ],
         compiler_params=pltpu.CompilerParams(
@@ -561,15 +615,32 @@
     )(basis_t, grad, new_rows, first, second)
 
 
+def finish_kernel(*refs):
+    count = len(refs) // 2
+    for source, target in zip(refs[:count], refs[count:]):
+        target[...] = source[...]
+
+
+def finish(*arrays):
+    return pl.pallas_call(
+        finish_kernel,
+        out_shape=tuple(jax.ShapeDtypeStruct(a.shape, a.dtype) for a in arrays),
+        in_specs=[VMEM_SPEC] * len(arrays),
+        out_specs=(VMEM_SPEC,) * len(arrays),
+        compiler_params=pltpu.CompilerParams(vmem_limit_bytes=8 << 20),
+        name="finish",
+    )(*arrays)
+
+
 def body(grad_partial, factors, bases, first_moment, second_moment):
-    all_grad, all_factor, all_basis = collect(grad_partial[0], factors[0].astype(BF16), bases[0])
+    all_grad, all_factor, all_basis = collect(grad_partial[0], factors[0], bases[0])
     whole = (BLOCK, BLOCK)
     all_grad = all_grad.reshape(whole)
     new_factor, basis_t, new_rows = refresh(
         all_grad, all_factor.reshape(whole), all_basis.reshape(whole), factors[0]
     )
-    first_new, second_new, direction = rotate(
-        basis_t, all_grad, new_rows, first_moment[0], second_moment[0]
+    first_new, second_new, direction = finish(
+        *rotate(basis_t, all_grad, new_rows, first_moment[0], second_moment[0])
     )
     return (new_factor[None], new_rows[None], first_new[None], second_new[None], direction[None])
 

time: 207 us -> 161 us (0.78)
  Pallas kernels: 200 us -> 156 us
    pallas_call x1, Pallas kernels: 91.6 us -> 57.1 us  [refresh(): pl.pallas_call(refresh_kernel, out_shape=(jax.ShapeDtypeStruct((ROWS, BLO...]
    pallas_call x1, Pallas kernels: 71 us -> 65.4 us  [collect(): pl.pallas_call(collect_kernel, out_shape=(jax.ShapeDtypeStruct((slots, RO...]
    pallas_call x1, Pallas kernels: 36.9 us -> 32.6 us  [rotate(): pl.pallas_call(rotate_kernel, out_shape=(jax.ShapeDtypeStruct((ROWS, HALF...]
    unnamed x3 -> x14, local copies, waits for them, and re-layouts: 4.61 us -> 4.4 us
where the time goes in v2:
time: 161 us
  Pallas kernels  156 us (97%)
  local copies, waits for them, and re-layouts  4.4 us (3%)
    pallas_call x1, Pallas kernels, collect(): pl.pallas_call(collect_kernel, out_shape=(jax.ShapeDtypeStruct((slots, RO...  65.4 us
    pallas_call x1, Pallas kernels, refresh(): pl.pallas_call(refresh_kernel, out_shape=(jax.ShapeDtypeStruct((ROWS, BLO...  57.1 us
    pallas_call x1, Pallas kernels, rotate(): pl.pallas_call(rotate_kernel, out_shape=(jax.ShapeDtypeStruct((ROWS, HALF...  32.6 us
    unnamed x14, local copies, waits for them, and re-layouts  4.4 us

profile of v2, /device:TPU:1, one launch (start us, length us, event | category | flops | bytes accessed | tf_op | source)
XLA Modules:
  0.0 160.9 jit_solution(17332162860563730728)
XLA Ops:
  0.6 0.0 copy-start
  0.6 1.6 copy-done
  2.2 0.0 copy-start.1
  2.2 0.9 copy-done.1
  3.2 0.0 copy-start.3
  3.2 0.9 copy-done.3
  4.1 0.0 copy-start.2
  4.1 65.4 %collect.1 = (bf16[16,64,1024]{2,1,0:T(8,128)(2,1)S(1)}, bf16[16,64,1024]{2,1,0:T(8,128)(2,1)S(1)}, f32[16,64,1024]{2,1,0:T(8,128)S(1)}) custom-call(bf16[2,64,8192]{2,1,0:T(8,128)(2,1)S(1)} %bitcast.16, f32[64,1024]{1,0:T(8,128)S(1)} %bitcast.18, f32[64,1024]{1,0:T(8,128)S(1)} %bitcast.20), custom_call_target="tpu_custom_call" | custom-call | tf_op jit(solution)/shard_map/collect/pallas_call | solution.py:290
  69.5 0.0 copy-done.2
  69.5 0.0 copy-start.4
  69.5 0.0 copy-start.5
  69.5 57.1 %refresh.1 = (f32[64,1024]{1,0:T(8,128)}, bf16[1024,1024]{1,0:T(8,128)(2,1)S(1)}, bf16[64,1024]{1,0:T(8,128)(2,1)}) custom-call(bf16[1024,1024]{1,0:T(8,128)(2,1)S(1)} %bitcast.13, bf16[1024,1024]{1,0:T(8,128)(2,1)S(1)} %bitcast.17, f32[1024,1024]{1,0:T(8,128)S(1)} %bitcast.15, f32[64,1024]{1,0:T(8,128)S(1)} %bitcast.19), custom_call_target="tpu_custom_call" | custom-call | tf_op jit(solution)/shard_map/refresh/pallas_call | solution.py:463
  126.7 0.0 copy-done.4
  126.7 0.0 copy-done.5
  126.7 0.0 copy-start.6
  126.7 0.9 copy-done.6
  127.6 32.6 %rotate.1 = (f32[64,512]{1,0:T(8,128)S(1)}, f32[64,512]{1,0:T(8,128)S(1)}, bf16[64,512]{1,0:T(8,128)(2,1)S(1)}) custom-call(bf16[1024,1024]{1,0:T(8,128)(2,1)S(1)} %get-tuple-element.22.basis_t, bf16[1024,1024]{1,0:T(8,128)(2,1)S(1)} %bitcast.14, bf16[64,1024]{1,0:T(8,128)(2,1)S(1)} %copy-done.6, f32[64,512]{1,0:T(8,128)S(1)} %bitcast.21, f32[64,512]{1,0:T(8,128)S(1)} %bitcast.22), custom_call_target="tpu_custom_call" | custom-call | tf_op jit(solution)/shard_map/rotate/pallas_call | solution.py:586
  160.2 0.7 finish.1
Async XLA Ops:
  0.6 1.6 copy-start
  2.2 0.9 copy-start.1
  3.2 0.9 copy-start.3
  4.1 65.4 %copy-start.2 = (f32[1,64,1024]{2,1,0:T(8,128)S(1)}, f32[1,64,1024]{2,1,0:T(8,128)}, u32[]{:S(2)}) copy-start(f32[1,64,1024]{2,1,0:T(8,128)} %param.6) | copy-start | bytes 786436
  69.5 57.2 %copy-start.4 = (f32[1,64,512]{2,1,0:T(8,128)S(1)}, f32[1,64,512]{2,1,0:T(8,128)}, u32[]{:S(2)}) copy-start(f32[1,64,512]{2,1,0:T(8,128)} %param.8) | copy-start | bytes 393220
  69.5 57.2 %copy-start.5 = (f32[1,64,512]{2,1,0:T(8,128)S(1)}, f32[1,64,512]{2,1,0:T(8,128)}, u32[]{:S(2)}) copy-start(f32[1,64,512]{2,1,0:T(8,128)} %param.9) | copy-start | bytes 393220
  126.7 0.9 copy-start.6

commit v3 on v2

--- a/solution.py
+++ b/solution.py
@@ -19,6 +19,7 @@
 CHUNKS = 4
 CROWS = ROWS // CHUNKS
 PANEL = 128
+WINDOW = 5 * PANEL
 VMEM_SPEC = pl.BlockSpec(memory_space=pltpu.VMEM)
 VMEM_BYTES = 40 << 20
 
@@ -143,8 +144,8 @@
 
 
 def collect_kernel(
-    grad, factor, basis, all_grad, all_factor, all_basis,
-    first_right, first_left, sum_right, sum_left,
+    grad_hbm, factor_hbm, basis_hbm, all_grad, all_factor, all_basis,
+    grad, factor, basis, first_right, first_left, sum_right, sum_left,
     right_a, right_b, left_a, left_b, lane_sum, lane_in, half_out,
     own_sem,
     s1, r1, s2, r2, s3, r3, ys, yr, ex_send, ex_recv,
@@ -164,7 +165,14 @@
         (dp, lax.rem(z + NZ - 1, NZ) * 2 + core),
         (dp, z * 2 + 1 - core),
     ]
+    staged = [
+        pltpu.make_async_copy(src, dst, own_sem.at[i])
+        for i, (src, dst) in enumerate(((grad_hbm, grad), (basis_hbm, basis), (factor_hbm, factor)))
+    ]
+    for copy in staged:
+        copy.start()
     meet(peers)
+    staged[0].wait()
 
     def region(owner, part, chunk):
         owner = lax.rem(owner + NX, NX)
@@ -181,15 +189,18 @@
     for r in range(CHUNKS):
         begin(remote(grad.at[region(x + 2, 0, r)], first_right.at[r], s1.at[r, 0], r1.at[r, 0], right, me))
         begin(remote(grad.at[region(x - 2, 1, r)], first_left.at[r], s1.at[r, 1], r1.at[r, 1], left, me))
-    own_basis = pltpu.make_async_copy(basis, all_basis.at[me], own_sem)
-    own_basis.start()
-    all_factor[me] = factor[...].astype(BF16)
-    gather_b = Gather(basis, all_basis, *gather_sems[0:4])
+    gather_b = Gather(None, all_basis, *gather_sems[0:4])
     gather_f = Gather(None, all_factor, *gather_sems[4:8])
     gather_g = [
         Gather(None, all_grad, *gather_sems[8 + 4 * h:12 + 4 * h], 2 * h * CROWS, 2 * CROWS) for h in range(2)
     ]
+    staged[1].wait()
+    all_basis[me] = basis[...].astype(BF16)
     gather_b.begin()
+    staged[2].wait()
+    for block in range(WINDOW // PANEL):
+        start = pl.multiple_of(lax.rem(z + block, NZ) * PANEL, PANEL)
+        all_factor[me, :, block * PANEL:(block + 1) * PANEL] = factor[:, pl.ds(start, PANEL)]
     gather_f.begin()
 
     def forward(r):
@@ -248,33 +259,32 @@
 
     forward(0)
     forward(1)
+    gather_b.advance(1)
     forward(2)
-    gather_b.advance(1)
     forward(3)
+    gather_f.advance(1)
     turn(0)
-    gather_f.advance(1)
+    gather_b.advance(2)
     turn(1)
+    gather_f.advance(2)
     turn(2)
-    gather_b.advance(2)
+    gather_b.advance(3)
     turn(3)
-    gather_f.advance(2)
+    gather_f.advance(3)
     land(0)
-    gather_b.advance(3)
+    gather_b.advance(4)
     paired(0)
+    gather_f.advance(4)
+    gather_g[0].advance(1)
     land(1)
-    gather_g[0].advance(1)
+    gather_g[0].advance(2)
     paired(1)
-    gather_f.advance(3)
-    gather_g[0].advance(2)
+    gather_g[0].advance(3)
     gather_g[1].advance(1)
-    gather_b.advance(4)
-    gather_f.advance(4)
-    gather_g[0].advance(3)
+    gather_g[0].advance(4)
     gather_g[1].advance(2)
-    gather_g[0].advance(4)
     gather_g[1].advance(3)
     gather_g[1].advance(4)
-    own_basis.wait()
     gather_b.finish()
     gather_f.finish()
     gather_g[0].finish()
@@ -291,17 +301,22 @@
         collect_kernel,
         out_shape=(
             jax.ShapeDtypeStruct((slots, ROWS, BLOCK), BF16),
+            jax.ShapeDtypeStruct((slots, ROWS, WINDOW), F32),
             jax.ShapeDtypeStruct((slots, ROWS, BLOCK), BF16),
-            jax.ShapeDtypeStruct((slots, ROWS, BLOCK), F32),
         ),
-        in_specs=[VMEM_SPEC] * 3,
+        in_specs=[pl.BlockSpec(memory_space=pltpu.HBM)] * 3,
         out_specs=(VMEM_SPEC,) * 3,
-        scratch_shapes=[chunk] * 8
+        scratch_shapes=[
+            pltpu.VMEM(grad.shape, BF16),
+            pltpu.VMEM(factor.shape, F32),
+            pltpu.VMEM(basis.shape, F32),
+        ]
+        + [chunk] * 8
         + [
             pltpu.VMEM((NY, ROWS, HALF), BF16),
             pltpu.VMEM((NY - 1, ROWS, HALF), BF16),
             pltpu.VMEM((ROWS, HALF), BF16),
-            dma(()),
+            dma((3,)),
         ]
         + [dma((CHUNKS, 2))] * 6
         + [dma((NY - 1, 2))] * 2
@@ -311,7 +326,7 @@
             collective_id=0, has_side_effects=True, vmem_limit_bytes=VMEM_BYTES
         ),
         name="collect",
-    )(grad, factor, basis)
+    )(*(pltpu.with_memory_space_constraint(a, pltpu.HBM) for a in (grad, factor, basis)))
 
 
 def split(value):
@@ -407,16 +422,23 @@
     mine = pl.ds(pl.multiple_of(me * ROWS, ROWS), ROWS)
     new_factor[...] = 0.95 * own_factor[...] + 0.05 * power[mine, :]
 
-    @pl.loop(0, BLOCK // PANEL)
+    @pl.loop(0, NZ)
     def _(i):
         rows = pl.ds(pl.multiple_of(i * PANEL, PANEL), PANEL)
-        now = 0.95 * factor[rows, :].astype(F32) + 0.05 * power[rows, :]
-        high[rows, :], low[rows, :] = split(now)
+        for block in range(WINDOW // PANEL):
+            columns = pl.ds(pl.multiple_of(lax.rem(i + block, NZ) * PANEL, PANEL), PANEL)
+            now = 0.95 * factor[rows, block * PANEL:(block + 1) * PANEL] + 0.05 * power[rows, columns]
+            high[rows, columns], low[rows, columns] = split(now)
+            if 0 < block < NZ // 2:
+                high[columns, rows], low[columns, rows] = split(now.T)
 
     @pl.loop(0, BLOCK // tile)
     def _(i):
         rows = pl.ds(pl.multiple_of(i * tile, tile), tile)
-        power[rows, :] = dot3(split(basis[:, rows]), (high[...], low[...]), TN)
+        now = basis[:, rows]
+        power[rows, :] = lax.dot_general(
+            now, high[...], TN, preferred_element_type=F32
+        ) + lax.dot_general(now, low[...], TN, preferred_element_type=F32)
 
     def factored(dst, corner):
         rows = [gram[corner + 8 * i:corner + 8 * i + 8, corner:corner + PANEL] for i in range(PANEL // 8)]
@@ -637,10 +659,10 @@
     whole = (BLOCK, BLOCK)
     all_grad = all_grad.reshape(whole)
     new_factor, basis_t, new_rows = refresh(
-        all_grad, all_factor.reshape(whole), all_basis.reshape(whole), factors[0]
+        all_grad, all_factor.reshape(BLOCK, WINDOW), all_basis.reshape(whole), factors[0]
     )
-    first_new, second_new, direction = finish(
-        *rotate(basis_t, all_grad, new_rows, first_moment[0], second_moment[0])
+    first_new, second_new, direction, new_rows = finish(
+        *rotate(basis_t, all_grad, new_rows, first_moment[0], second_moment[0]), new_rows
     )
     return (new_factor[None], new_rows[None], first_new[None], second_new[None], direction[None])
 

time: 161 us -> 157 us (0.975)
  local copies, waits for them, and re-layouts: 4.4 us -> 0.02 us
    unnamed x14 -> x6, local copies, waits for them, and re-layouts: 4.4 us -> 0.02 us
    pallas_call x1, Pallas kernels: 57.1 us -> 55.5 us  [refresh(): pl.pallas_call(refresh_kernel, out_shape=(jax.ShapeDtypeStruct((ROWS, BLO...]
    pallas_call x1, Pallas kernels: 65.4 us -> 67 us  [collect(): pl.pallas_call(collect_kernel, out_shape=(jax.ShapeDtypeStruct((slots, RO...]
where the time goes in v3:
time: 157 us
  Pallas kernels  156 us (99%)
    pallas_call x1, Pallas kernels, collect(): pl.pallas_call(collect_kernel, out_shape=(jax.ShapeDtypeStruct((slots, RO...  67 us
    pallas_call x1, Pallas kernels, refresh(): pl.pallas_call(refresh_kernel, out_shape=(jax.ShapeDtypeStruct((ROWS, BLO...  55.5 us
    pallas_call x1, Pallas kernels, rotate(): pl.pallas_call(rotate_kernel, out_shape=(jax.ShapeDtypeStruct((ROWS, HALF...  32.6 us

profile of v3, /device:TPU:1, one launch (start us, length us, event | category | flops | bytes accessed | tf_op | source)
XLA Modules:
  0.0 156.5 jit_solution(15817901623535915475)
XLA Ops:
  0.6 0.0 copy-start
  0.6 67.0 %collect.1 = (bf16[16,64,1024]{2,1,0:T(8,128)(2,1)S(1)}, f32[16,64,640]{2,1,0:T(8,128)S(1)}, bf16[16,64,1024]{2,1,0:T(8,128)(2,1)S(1)}) custom-call(bf16[2,64,8192]{2,1,0:T(8,128)(2,1)} %bitcast.21, f32[64,1024]{1,0:T(8,128)} %bitcast.17, f32[64,1024]{1,0:T(8,128)} %bitcast.22), custom_call_target="tpu_custom_call" | custom-call | tf_op jit(solution)/shard_map/collect/pallas_call | solution.py:300
  67.6 0.0 copy-done
  67.6 0.0 copy-start.1
  67.7 0.0 copy-start.2
  67.7 55.5 %refresh.1 = (f32[64,1024]{1,0:T(8,128)}, bf16[1024,1024]{1,0:T(8,128)(2,1)S(1)}, bf16[64,1024]{1,0:T(8,128)(2,1)S(1)}) custom-call(bf16[1024,1024]{1,0:T(8,128)(2,1)S(1)} %bitcast.13, f32[1024,640]{1,0:T(8,128)S(1)} %bitcast.15, bf16[1024,1024]{1,0:T(8,128)(2,1)S(1)} %bitcast.16, f32[64,1024]{1,0:T(8,128)S(1)} %bitcast.18), custom_call_target="tpu_custom_call" | custom-call | tf_op jit(solution)/shard_map/refresh/pallas_call | solution.py:485
  123.1 0.0 copy-done.1
  123.1 0.0 copy-done.2
  123.1 32.6 %rotate.1 = (f32[64,512]{1,0:T(8,128)S(1)}, f32[64,512]{1,0:T(8,128)S(1)}, bf16[64,512]{1,0:T(8,128)(2,1)S(1)}) custom-call(bf16[1024,1024]{1,0:T(8,128)(2,1)S(1)} %get-tuple-element.22.basis_t, bf16[1024,1024]{1,0:T(8,128)(2,1)S(1)} %bitcast.14, bf16[64,1024]{1,0:T(8,128)(2,1)S(1)} %get-tuple-element.23.new_rows.refs_3_, f32[64,512]{1,0:T(8,128)S(1)} %bitcast.19, ...), custom_call_target="tpu_custom_call" | custom-call | tf_op jit(solution)/shard_map/rotate/pallas_call | solution.py:608
  155.7 0.8 finish.1
Async XLA Ops:
  0.6 67.0 %copy-start = (f32[1,64,1024]{2,1,0:T(8,128)S(1)}, f32[1,64,1024]{2,1,0:T(8,128)}, u32[]{:S(2)}) copy-start(f32[1,64,1024]{2,1,0:T(8,128)} %param.6) | copy-start | bytes 786436
  67.6 55.5 %copy-start.1 = (f32[1,64,512]{2,1,0:T(8,128)S(1)}, f32[1,64,512]{2,1,0:T(8,128)}, u32[]{:S(2)}) copy-start(f32[1,64,512]{2,1,0:T(8,128)} %param.8) | copy-start | bytes 393220
  67.7 55.5 %copy-start.2 = (f32[1,64,512]{2,1,0:T(8,128)S(1)}, f32[1,64,512]{2,1,0:T(8,128)}, u32[]{:S(2)}) copy-start(f32[1,64,512]{2,1,0:T(8,128)} %param.9) | copy-start | bytes 393220

commit v4 on v3

--- a/solution.py
+++ b/solution.py
@@ -41,7 +41,7 @@
     )
 
 
-def meet(peers):
+def greet(peers):
     barrier = pltpu.get_barrier_semaphore()
     for dp, fsdp in peers:
         pl.semaphore_signal(
@@ -50,7 +50,11 @@
             device_id={"dp": dp, "fsdp": fsdp},
             device_id_type=pl.DeviceIdType.MESH,
         )
-    pl.semaphore_wait(barrier, len(peers))
+    return lambda: pl.semaphore_wait(barrier, len(peers))
+
+
+def meet(peers):
+    greet(peers)()
 
 
 class Gather:
@@ -388,22 +392,46 @@
         if group + 2 < count:
             spread = [down(here, l) for l in range(8)]
             inside = (lane >= base) & (lane < base + 8)
-            for n in range(group + 2, count):
+            near = min(group + 3, count)
+            for n in range(group + 2, near):
                 terms = [along(rows[n], base + l) * spread[l] for l in range(8)]
                 while len(terms) > 1:
                     terms = [terms[i] + terms[i + 1] for i in range(0, len(terms), 2)]
                 rows[n] = jnp.where(inside, 0.0, rows[n]) - terms[0]
+            if near < count:
+                far = jnp.concatenate(rows[near:], axis=0)
+                lifted = [here if n == group else jnp.zeros(shape, F32) for n in range(count)]
+                change = dot3(split(far), split(jnp.concatenate(lifted, axis=0)), NN)
+                for n in range(near, count):
+                    rows[n] = jnp.where(inside, 0.0, rows[n]) - change[8 * (n - near):8 * (n - near) + 8]
     return done
 
 
 def refresh_kernel(
-    grad, factor, basis, own_factor, new_factor, basis_t, new_rows,
-    power, high, low, gram, upper, lower,
+    grad, factor, basis, own_factor, first_old, second_old,
+    new_factor, new_rows, new_first, new_second, direction,
+    power, high, low, gram, upper, lower, basis_t, right_top, right_low, slab, left_rows,
+    part, all_normal, weighted, weighted_in,
+    send, recv, *gather_sems,
 ):
     x, y, z, core = place()
     me = z * 2 + core
     side = lax.rem(y, 2)
     tile = 256
+    dp = x * NY + y
+    partner = dp + 1 - 2 * side
+    all_here = greet([
+        (partner, me),
+        (dp, lax.rem(z + 1, NZ) * 2 + core),
+        (dp, lax.rem(z + NZ - 1, NZ) * 2 + core),
+        (dp, z * 2 + 1 - core),
+    ])
+
+    def across(src, dst, i):
+        return remote(src, dst, send.at[i], recv.at[i], partner, me)
+
+    def dot(a, b, numbers):
+        return lax.dot_general(a, b, numbers, preferred_element_type=F32)
 
     @pl.when(side == 0)
     def _():
@@ -447,6 +475,17 @@
         return split(dst[...])
 
     top, bottom = slice(0, PANEL), slice(PANEL, 2 * PANEL)
+    to_slab = across(basis_t.at[mine], slab, 4)
+    to_rows = across(new_rows, left_rows, 5)
+
+    def to_left(k):
+        if k < 2:
+            rows = pl.ds(k * tile, tile)
+            return across(basis_t.at[rows], right_top.at[rows], k)
+        rows, target = pl.ds(k * tile, tile), pl.ds((k - 2) * tile, tile)
+        return across(basis_t.at[rows, 0:HALF], right_low.at[target], k)
+
+    all_here()
 
     @pl.loop(0, BLOCK // tile)
     def _(k):
@@ -464,6 +503,15 @@
         gram[bottom, bottom] = lower[...]
         fresh = dot3(split(gram[...]), panel, NN)
         basis_t[rows, :] = fresh.astype(BF16)
+        for panel_index in range(BLOCK // tile):
+            @pl.when((side == 1) & (k == panel_index))
+            def _():
+                to_left(panel_index).start()
+
+        @pl.when((side == 0) & (k == me // 4))
+        def _():
+            to_slab.start()
+
         fresh = split(fresh)
 
         @pl.loop(k + 1, BLOCK // tile)
@@ -481,16 +529,89 @@
     ).astype(BF16)
 
 
-def refresh(grad, factor, basis, own_factor):
+    count = ROWS // 2
+    halves = [pl.ds(h * count, count) for h in range(2)]
+    to_weighted = [across(weighted.at[r], weighted_in.at[r], 6 + h) for h, r in enumerate(halves)]
+    gathers = [
+        Gather(None, all_normal, *gather_sems[4 * h:4 * h + 4], h * count, count) for h in range(2)
+    ]
+
+    @pl.when(side == 0)
+    def _():
+        to_rows.start()
+        slab[...] = basis_t[mine, :]
+        left_rows[...] = new_rows[...]
+        mixed = dot(slab[...], grad[...], NN).astype(BF16)
+        to_left(0).wait_recv()
+        to_left(1).wait_recv()
+        part[...] = dot(mixed, right_top[...], NT)
+
+    @pl.when(side == 1)
+    def _():
+        to_slab.wait_recv()
+        mixed = dot(slab[...], grad[...], NN).astype(BF16)
+        part[...] = dot(mixed, basis_t[HALF:BLOCK, :], NT)
+
+    for h, rows in enumerate(halves):
+        rotated = part[rows, :]
+        first_now = 0.95 * first_old[rows, :] + 0.05 * rotated
+        second_now = 0.95 * second_old[rows, :] + 0.05 * rotated * rotated
+        all_normal[me, rows] = (first_now / (jnp.sqrt(second_now) + 1e-08)).astype(BF16)
+        gathers[h].begin()
+        new_first[rows, :] = first_now
+        new_second[rows, :] = second_now
+
+    for step in range(1, NZ // 2 + 1):
+        for gather in gathers:
+            gather.advance(step)
+    for gather in gathers:
+        gather.finish()
+
+    @pl.when(side == 1)
+    def _():
+        to_rows.wait_recv()
+
+    weighted[...] = dot(left_rows[...], all_normal[...].reshape(BLOCK, HALF), NN).astype(BF16)
+    for copy in to_weighted:
+        copy.start()
+
+    @pl.when(side == 0)
+    def _():
+        to_left(2).wait_recv()
+        to_left(3).wait_recv()
+        own = dot(weighted[...], right_top[:, 0:HALF], NN)
+        for copy in to_weighted:
+            copy.wait_recv()
+        direction[...] = (own + dot(weighted_in[...], right_low[...], NN)).astype(BF16)
+        to_slab.wait_send()
+        to_rows.wait_send()
+
+    @pl.when(side == 1)
+    def _():
+        own = dot(weighted[...], basis_t[HALF:BLOCK, HALF:BLOCK], NN)
+        for copy in to_weighted:
+            copy.wait_recv()
+        direction[...] = (own + dot(weighted_in[...], basis_t[0:HALF, HALF:BLOCK], NN)).astype(BF16)
+        for k in range(4):
+            to_left(k).wait_send()
+
+    for copy in to_weighted:
+        copy.wait_send()
+
+
+def refresh(grad, factor, basis, own_factor, first, second):
+    dma = pltpu.SemaphoreType.DMA
     return pl.pallas_call(
         refresh_kernel,
         out_shape=(
             jax.ShapeDtypeStruct((ROWS, BLOCK), F32),
-            jax.ShapeDtypeStruct((BLOCK, BLOCK), BF16),
             jax.ShapeDtypeStruct((ROWS, BLOCK), BF16),
+            jax.ShapeDtypeStruct((ROWS, HALF), F32),
+            jax.ShapeDtypeStruct((ROWS, HALF), F32),
+            jax.ShapeDtypeStruct((ROWS, HALF), BF16),
         ),
-        in_specs=[VMEM_SPEC] * 4,
-        out_specs=(VMEM_SPEC,) * 3,
+        in_specs=[VMEM_SPEC] * 6,
+        out_specs=(VMEM_SPEC,) * 5,
         scratch_shapes=[
             pltpu.VMEM((BLOCK, BLOCK), F32),
             pltpu.VMEM((BLOCK, BLOCK), BF16),
@@ -498,143 +619,25 @@
             pltpu.VMEM((2 * PANEL, 2 * PANEL), F32),
             pltpu.VMEM((PANEL, PANEL), F32),
             pltpu.VMEM((PANEL, PANEL), F32),
-        ],
-        compiler_params=pltpu.CompilerParams(vmem_limit_bytes=VMEM_BYTES),
-        name="refresh",
-    )(grad, factor, basis, own_factor)
-
-
-def rotate_kernel(
-    basis_t, grad, new_rows, first, second, new_first, new_second, direction,
-    mixed, mixed_in, left_rows, part, part_in, all_normal, weighted, weighted_in, turned, turned_in,
-    send, recv, *gather_sems,
-):
-    x, y, z, core = place()
-    me = z * 2 + core
-    side = lax.rem(y, 2)
-    dp = x * NY + y
-    partner = dp + 1 - 2 * side
-    meet([
-        (partner, me),
-        (dp, lax.rem(z + 1, NZ) * 2 + core),
-        (dp, lax.rem(z + NZ - 1, NZ) * 2 + core),
-        (dp, z * 2 + 1 - core),
-    ])
-
-    def across(src, dst, i):
-        return remote(src, dst, send.at[i], recv.at[i], partner, me)
-
-    def dot(a, b, numbers):
-        return lax.dot_general(a, b, numbers, preferred_element_type=F32)
-
-    count = ROWS // 2
-    halves = [pl.ds(h * count, count) for h in range(2)]
-    to_rows = across(new_rows, left_rows, 0)
-    to_mixed = [across(mixed.at[r], mixed_in.at[r], 1 + h) for h, r in enumerate(halves)]
-    to_part = [across(part.at[r], part_in.at[r], 3 + h) for h, r in enumerate(halves)]
-    to_weighted = [across(weighted.at[r], weighted_in.at[r], 5 + h) for h, r in enumerate(halves)]
-    to_turned = [across(turned.at[r], turned_in.at[r], 7 + h) for h, r in enumerate(halves)]
-    gathers = [
-        Gather(None, all_normal, *gather_sems[4 * h:4 * h + 4], h * count, count) for h in range(2)
-    ]
-    mine = pl.ds(pl.multiple_of(me * ROWS, ROWS), ROWS)
-
-    @pl.when(side == 0)
-    def _():
-        mixed[...] = dot(basis_t[mine, :], grad[...], NN).astype(BF16)
-        for copy in to_mixed:
-            copy.start()
-        to_rows.start()
-        left_rows[...] = new_rows[...]
-
-    for h, rows in enumerate(halves):
-        @pl.when(side == 0)
-        def _():
-            to_part[h].wait_recv()
-
-        @pl.when(side == 1)
-        def _():
-            to_mixed[h].wait_recv()
-            now = mixed_in[rows, :]
-            part[rows, :] = dot(now, basis_t[0:HALF, :], NT)
-            to_part[h].start()
-            part_in[rows, :] = dot(now, basis_t[HALF:BLOCK, :], NT)
-
-        rotated = part_in[rows, :]
-        first_now = 0.95 * first[rows, :] + 0.05 * rotated
-        second_now = 0.95 * second[rows, :] + 0.05 * rotated * rotated
-        all_normal[me, rows] = (first_now / (jnp.sqrt(second_now) + 1e-08)).astype(BF16)
-        gathers[h].begin()
-        new_first[rows, :] = first_now
-        new_second[rows, :] = second_now
-
-    @pl.when(side == 1)
-    def _():
-        to_rows.wait_recv()
-
-    for step in range(1, NZ // 2 + 1):
-        for gather in gathers:
-            gather.advance(step)
-    for gather in gathers:
-        gather.finish()
-    weighted[...] = dot(left_rows[...], all_normal[...].reshape(BLOCK, HALF), NN).astype(BF16)
-
-    @pl.when(side == 0)
-    def _():
-        for copy in to_weighted:
-            copy.start()
-        for h, rows in enumerate(halves):
-            to_turned[h].wait_recv()
-            direction[rows, :] = turned_in[rows, :]
-        for copy in [to_rows] + to_mixed + to_weighted:
-            copy.wait_send()
-
-    @pl.when(side == 1)
-    def _():
-        own = dot(weighted[...], basis_t[HALF:BLOCK, :], NN)
-        for h, rows in enumerate(halves):
-            to_weighted[h].wait_recv()
-            total = own[h * count:(h + 1) * count] + dot(weighted_in[rows, :], basis_t[0:HALF, :], NN)
-            total = total.astype(BF16)
-            turned[rows, :] = total[:, 0:HALF]
-            to_turned[h].start()
-            direction[rows, :] = total[:, HALF:BLOCK]
-        for copy in to_part + to_turned:
-            copy.wait_send()
-
-
-def rotate(basis_t, grad, new_rows, first, second):
-    dma = pltpu.SemaphoreType.DMA
-    return pl.pallas_call(
-        rotate_kernel,
-        out_shape=(
-            jax.ShapeDtypeStruct((ROWS, HALF), F32),
-            jax.ShapeDtypeStruct((ROWS, HALF), F32),
-            jax.ShapeDtypeStruct((ROWS, HALF), BF16),
-        ),
-        in_specs=[VMEM_SPEC] * 5,
-        out_specs=(VMEM_SPEC,) * 3,
-        scratch_shapes=[
+            pltpu.VMEM((BLOCK, BLOCK), BF16),
+            pltpu.VMEM((HALF, BLOCK), BF16),
+            pltpu.VMEM((HALF, HALF), BF16),
             pltpu.VMEM((ROWS, BLOCK), BF16),
             pltpu.VMEM((ROWS, BLOCK), BF16),
-            pltpu.VMEM((ROWS, BLOCK), BF16),
-            pltpu.VMEM((ROWS, HALF), F32),
             pltpu.VMEM((ROWS, HALF), F32),
             pltpu.VMEM((2 * NZ, ROWS, HALF), BF16),
             pltpu.VMEM((ROWS, HALF), BF16),
             pltpu.VMEM((ROWS, HALF), BF16),
-            pltpu.VMEM((ROWS, HALF), BF16),
-            pltpu.VMEM((ROWS, HALF), BF16),
-            dma((9,)),
-            dma((9,)),
+            dma((8,)),
+            dma((8,)),
             *GATHER_SEMS,
             *GATHER_SEMS,
         ],
         compiler_params=pltpu.CompilerParams(
             collective_id=1, has_side_effects=True, vmem_limit_bytes=VMEM_BYTES
         ),
-        name="rotate",
-    )(basis_t, grad, new_rows, first, second)
+        name="refresh",
+    )(grad, factor, basis, own_factor, first, second)
 
 
 def finish_kernel(*refs):
@@ -658,11 +661,11 @@
     all_grad, all_factor, all_basis = collect(grad_partial[0], factors[0], bases[0])
     whole = (BLOCK, BLOCK)
     all_grad = all_grad.reshape(whole)
-    new_factor, basis_t, new_rows = refresh(
-        all_grad, all_factor.reshape(BLOCK, WINDOW), all_basis.reshape(whole), factors[0]
-    )
-    first_new, second_new, direction, new_rows = finish(
-        *rotate(basis_t, all_grad, new_rows, first_moment[0], second_moment[0]), new_rows
+    new_factor, new_rows, first_new, second_new, direction = finish(
+        *refresh(
+            all_grad, all_factor.reshape(BLOCK, WINDOW), all_basis.reshape(whole),
+            factors[0], first_moment[0], second_moment[0],
+        )
     )
     return (new_factor[None], new_rows[None], first_new[None], second_new[None], direction[None])
 

time: 157 us -> 146 us (0.930)
  Pallas kernels: 156 us -> 145 us
    pallas_call x1 -> x0, Pallas kernels: 32.6 us -> none  [rotate(): pl.pallas_call(rotate_kernel, out_shape=(jax.ShapeDtypeStruct((ROWS, HALF...]
    pallas_call x1, Pallas kernels: 55.5 us -> 77.1 us  [refresh(): pl.pallas_call(refresh_kernel, out_shape=(jax.ShapeDtypeStruct((ROWS, BLO...]
where the time goes in v4:
time: 146 us
  Pallas kernels  145 us (99%)
    pallas_call x1, Pallas kernels, refresh(): pl.pallas_call(refresh_kernel, out_shape=(jax.ShapeDtypeStruct((ROWS, BLO...  77.1 us
    pallas_call x1, Pallas kernels, collect(): pl.pallas_call(collect_kernel, out_shape=(jax.ShapeDtypeStruct((slots, RO...  67 us

profile of v4, /device:TPU:1, one launch (start us, length us, event | category | flops | bytes accessed | tf_op | source)
XLA Modules:
  0.0 145.6 jit_solution(5223338045203218080)
XLA Ops:
  0.6 0.0 copy-start.2
  0.6 0.0 copy-start.1
  0.7 0.0 copy-start
  0.7 67.0 %collect.1 = (bf16[16,64,1024]{2,1,0:T(8,128)(2,1)S(1)}, f32[16,64,640]{2,1,0:T(8,128)S(1)}, bf16[16,64,1024]{2,1,0:T(8,128)(2,1)S(1)}) custom-call(bf16[2,64,8192]{2,1,0:T(8,128)(2,1)} %bitcast.20, f32[64,1024]{1,0:T(8,128)} %bitcast.16, f32[64,1024]{1,0:T(8,128)} %bitcast.21), custom_call_target="tpu_custom_call" | custom-call | tf_op jit(solution)/shard_map/collect/pallas_call | solution.py:304
  67.7 0.0 copy-done.2
  67.7 0.0 copy-done.1
  67.7 0.0 copy-done
  67.7 77.1 %refresh.1 = (f32[64,1024]{1,0:T(8,128)S(1)}, bf16[64,1024]{1,0:T(8,128)(2,1)S(1)}, f32[64,512]{1,0:T(8,128)S(1)}, f32[64,512]{1,0:T(8,128)S(1)}, bf16[64,512]{1,0:T(8,128)(2,1)S(1)}) custom-call(bf16[1024,1024]{1,0:T(8,128)(2,1)S(1)} %bitcast.14, f32[1024,640]{1,0:T(8,128)S(1)} %bitcast.13, bf16[1024,1024]{1,0:T(8,128)(2,1)S(1)} %bitcast.15, ...), custom_call_target="tpu_custom_call" | custom-call | tf_op jit(solution)/shard_map/refresh/pallas_call | solution.py:604
  144.7 0.9 finish.1
Async XLA Ops:
  0.6 67.0 %copy-start.2 = (f32[1,64,512]{2,1,0:T(8,128)S(1)}, f32[1,64,512]{2,1,0:T(8,128)}, u32[]{:S(2)}) copy-start(f32[1,64,512]{2,1,0:T(8,128)} %param.9) | copy-start | bytes 393220
  0.6 67.0 %copy-start.1 = (f32[1,64,512]{2,1,0:T(8,128)S(1)}, f32[1,64,512]{2,1,0:T(8,128)}, u32[]{:S(2)}) copy-start(f32[1,64,512]{2,1,0:T(8,128)} %param.8) | copy-start | bytes 393220
  0.7 67.0 %copy-start = (f32[1,64,1024]{2,1,0:T(8,128)S(1)}, f32[1,64,1024]{2,1,0:T(8,128)}, u32[]{:S(2)}) copy-start(f32[1,64,1024]{2,1,0:T(8,128)} %param.6) | copy-start | bytes 786436

commit v5 on v4

--- a/solution.py
+++ b/solution.py
@@ -18,6 +18,7 @@
 HALF = 512
 CHUNKS = 4
 CROWS = ROWS // CHUNKS
+PARTS = ((0, 3 * CROWS), (3 * CROWS, CROWS))
 PANEL = 128
 WINDOW = 5 * PANEL
 VMEM_SPEC = pl.BlockSpec(memory_space=pltpu.VMEM)
@@ -67,12 +68,15 @@
         self.dp = self.x * NY + self.y
         self.started = []
 
+    def ways(self, step):
+        return (0, 1) if step < NZ // 2 or self.count % (2 * CROWS) == 0 else (0,)
+
     def slot(self, z, core):
         return lax.rem(z + NZ, NZ) * 2 + core
 
     def part(self, z, core, step, way):
         start, count = self.start, self.count
-        if step == NZ // 2:
+        if len(self.ways(step)) == 2 and step == NZ // 2:
             count = count // 2
             start = start + way * count
         return self.held.at[self.slot(z, core), pl.ds(start, count)]
@@ -108,7 +112,7 @@
         self.started.append(copy)
 
     def advance(self, step):
-        for way in range(2):
+        for way in self.ways(step):
             sign = 1 - 2 * way
             view = self.part(self.z - sign * step, self.core, step, way)
             remote(
@@ -119,7 +123,7 @@
                 self.dp,
                 self.slot(self.z + sign, self.core),
             ).wait_recv()
-            if step < NZ // 2:
+            if step < NZ // 2 and way in self.ways(step + 1):
                 copy = self.hop(step + 1, way)
                 copy.start()
                 self.started.append(copy)
@@ -131,7 +135,7 @@
         other = 1 - self.core
         self.hand(0, self.part(self.z, other, 1, 0), other).wait_recv()
         for step in range(1, NZ // 2 + 1):
-            for way in range(2):
+            for way in self.ways(step):
                 sign = 1 - 2 * way
                 view = self.part(self.z - sign * step, other, step, way)
                 self.hand(1 + 2 * (step - 1) + way, view, other).wait_recv()
@@ -196,7 +200,7 @@
     gather_b = Gather(None, all_basis, *gather_sems[0:4])
     gather_f = Gather(None, all_factor, *gather_sems[4:8])
     gather_g = [
-        Gather(None, all_grad, *gather_sems[8 + 4 * h:12 + 4 * h], 2 * h * CROWS, 2 * CROWS) for h in range(2)
+        Gather(None, all_grad, *gather_sems[8 + 4 * h:12 + 4 * h], *PARTS[h]) for h in range(2)
     ]
     staged[1].wait()
     all_basis[me] = basis[...].astype(BF16)
@@ -231,24 +235,23 @@
             total = total.astype(BF16)
             for piece in range(4):
                 lane_sum[part * 4 + piece, rows] = total[:, piece * HALF:(piece + 1) * HALF]
-        if r % 2:
-            send_rows = pl.ds((r - 1) * CROWS, 2 * CROWS)
-            for d in range(1, NY):
-                target = lax.rem(y + d, NY)
-                begin(remote(
-                    lane_sum.at[target, send_rows], lane_in.at[d - 1, send_rows],
-                    ys.at[d - 1, r // 2], yr.at[d - 1, r // 2], x * NY + target, me,
-                ))
+        for d in range(1, NY):
+            target = lax.rem(y + d, NY)
+            begin(remote(
+                lane_sum.at[target, rows], lane_in.at[d - 1, rows],
+                ys.at[d - 1, r], yr.at[d - 1, r], x * NY + target, me,
+            ))
 
     mine = pl.ds(pl.multiple_of(side * HALF, HALF), HALF)
     theirs = pl.ds(pl.multiple_of((1 - side) * HALF, HALF), HALF)
 
     def land(h):
-        rows = pl.ds(2 * h * CROWS, 2 * CROWS)
+        rows = pl.ds(*PARTS[h])
         total = lane_sum[y, rows].astype(F32)
-        for d in range(1, NY):
-            view = lane_in.at[d - 1, rows]
-            remote(view, view, ys.at[d - 1, h], yr.at[d - 1, h], x * NY + lax.rem(y + d, NY), me).wait_recv()
+        for r in range(PARTS[h][0] // CROWS, sum(PARTS[h]) // CROWS):
+            for d in range(1, NY):
+                view = lane_in.at[d - 1, pl.ds(r * CROWS, CROWS)]
+                remote(view, view, ys.at[d - 1, r], yr.at[d - 1, r], x * NY + lax.rem(y + d, NY), me).wait_recv()
         for d in range(1, NY):
             total = total + lane_in[d - 1, rows].astype(F32)
         total = total.astype(BF16)
@@ -257,7 +260,7 @@
         begin(remote(half_out.at[rows], all_grad.at[me, rows, mine], ex_send.at[h], ex_recv.at[h], partner, me))
 
     def paired(h):
-        view = all_grad.at[me, pl.ds(2 * h * CROWS, 2 * CROWS), theirs]
+        view = all_grad.at[me, pl.ds(*PARTS[h]), theirs]
         remote(view, view, ex_send.at[h], ex_recv.at[h], partner, me).wait_recv()
         gather_g[h].begin()
 
@@ -278,17 +281,12 @@
     land(0)
     gather_b.advance(4)
     paired(0)
+    land(1)
     gather_f.advance(4)
-    gather_g[0].advance(1)
-    land(1)
-    gather_g[0].advance(2)
     paired(1)
-    gather_g[0].advance(3)
-    gather_g[1].advance(1)
-    gather_g[0].advance(4)
-    gather_g[1].advance(2)
-    gather_g[1].advance(3)
-    gather_g[1].advance(4)
+    for step in range(1, NZ // 2 + 1):
+        gather_g[0].advance(step)
+        gather_g[1].advance(step)
     gather_b.finish()
     gather_f.finish()
     gather_g[0].finish()
@@ -323,7 +321,7 @@
             dma((3,)),
         ]
         + [dma((CHUNKS, 2))] * 6
-        + [dma((NY - 1, 2))] * 2
+        + [dma((NY - 1, CHUNKS))] * 2
         + [dma((2,))] * 2
         + list(GATHER_SEMS) * 4,
         compiler_params=pltpu.CompilerParams(

time: 146 us -> 139 us (0.952)
  Pallas kernels: 145 us -> 138 us
    pallas_call x1, Pallas kernels: 67 us -> 61.6 us  [collect(): pl.pallas_call(collect_kernel, out_shape=(jax.ShapeDtypeStruct((slots, RO...]
where the time goes in v5:
time: 139 us
  Pallas kernels  138 us (99%)
    pallas_call x1, Pallas kernels, refresh(): pl.pallas_call(refresh_kernel, out_shape=(jax.ShapeDtypeStruct((ROWS, BLO...  75.7 us
    pallas_call x1, Pallas kernels, collect(): pl.pallas_call(collect_kernel, out_shape=(jax.ShapeDtypeStruct((slots, RO...  61.6 us

profile of v5, /device:TPU:1, one launch (start us, length us, event | category | flops | bytes accessed | tf_op | source)
XLA Modules:
  0.0 138.8 jit_solution(8598035287025537984)
XLA Ops:
  0.6 0.0 copy-start.2
  0.6 0.0 copy-start.1
  0.7 0.0 copy-start
  0.7 61.6 %collect.1 = (bf16[16,64,1024]{2,1,0:T(8,128)(2,1)S(1)}, f32[16,64,640]{2,1,0:T(8,128)S(1)}, bf16[16,64,1024]{2,1,0:T(8,128)(2,1)S(1)}) custom-call(bf16[2,64,8192]{2,1,0:T(8,128)(2,1)} %bitcast.20, f32[64,1024]{1,0:T(8,128)} %bitcast.16, f32[64,1024]{1,0:T(8,128)} %bitcast.21), custom_call_target="tpu_custom_call" | custom-call | tf_op jit(solution)/shard_map/collect/pallas_call | solution.py:302
  62.2 0.0 copy-done.2
  62.3 0.0 copy-done.1
  62.3 0.0 copy-done
  62.3 75.7 %refresh.1 = (f32[64,1024]{1,0:T(8,128)S(1)}, bf16[64,1024]{1,0:T(8,128)(2,1)S(1)}, f32[64,512]{1,0:T(8,128)S(1)}, f32[64,512]{1,0:T(8,128)S(1)}, bf16[64,512]{1,0:T(8,128)(2,1)S(1)}) custom-call(bf16[1024,1024]{1,0:T(8,128)(2,1)S(1)} %bitcast.14, f32[1024,640]{1,0:T(8,128)S(1)} %bitcast.13, bf16[1024,1024]{1,0:T(8,128)(2,1)S(1)} %bitcast.15, ...), custom_call_target="tpu_custom_call" | custom-call | tf_op jit(solution)/shard_map/refresh/pallas_call | solution.py:602
  137.9 0.9 finish.1
Async XLA Ops:
  0.6 61.6 %copy-start.2 = (f32[1,64,512]{2,1,0:T(8,128)S(1)}, f32[1,64,512]{2,1,0:T(8,128)}, u32[]{:S(2)}) copy-start(f32[1,64,512]{2,1,0:T(8,128)} %param.9) | copy-start | bytes 393220
  0.6 61.6 %copy-start.1 = (f32[1,64,512]{2,1,0:T(8,128)S(1)}, f32[1,64,512]{2,1,0:T(8,128)}, u32[]{:S(2)}) copy-start(f32[1,64,512]{2,1,0:T(8,128)} %param.8) | copy-start | bytes 393220
  0.7 61.6 %copy-start = (f32[1,64,1024]{2,1,0:T(8,128)S(1)}, f32[1,64,1024]{2,1,0:T(8,128)}, u32[]{:S(2)}) copy-start(f32[1,64,1024]{2,1,0:T(8,128)} %param.6) | copy-start | bytes 786436
